TPU v7x, 32 devices: a whole 2x2x4 slice. The times are simulated.
32 devices in a mesh: segment: 2 (over x), expert: 16 (over z, y, core).
Axes of the slice: x: 2, y: 2, z: 4, core: 2. Of those that a mesh axis runs over, the one named last changes fastest.
Arguments:
- handoff: bfloat16 [2, 1024, 4096], P('segment', 'expert'), may hold values from -6 to 6
- saved_inputs: bfloat16 [2, 1024, 4096], P('segment', 'expert'), may hold values from -6 to 6
- cotangent: bfloat16 [2, 1024, 4096], P('segment', 'expert'), may hold values from -6 to 6
- ids_forward: int32 [2, 1024, 2], P('segment', 'expert'), may hold values from 0 to 63, all different within a row; in each aligned block of 64 rows (0 to 63, 64 to 127, ..., all dimensions but the last counted through in order) at most 5 rows name the same one
- gates_forward: float32 [2, 1024, 2], P('segment', 'expert'), may hold values from 0.25 to 1
- ids_backward: int32 [2, 1024, 2], P('segment', 'expert'), may hold values from 0 to 63, all different within a row; in each aligned block of 64 rows (0 to 63, 64 to 127, ..., all dimensions but the last counted through in order) at most 5 rows name the same one
- gates_backward: float32 [2, 1024, 2], P('segment', 'expert'), may hold values from 0.25 to 1
- weight_in: bfloat16 [2, 4096, 2048], P('segment', None, 'expert'), may hold values from -0.09375 to 0.09375
- weight_out: bfloat16 [2, 2048, 4096], P('segment', 'expert'), may hold values from -0.125 to 0.125
Outputs:
- expert_mix: bfloat16 [2, 1024, 4096], P('segment', 'expert')
- input_grads: bfloat16 [2, 1024, 4096], P('segment', 'expert')
Inputs may be any that keep to these rules, and one draw needn't show every extreme that they name: `ids_forward`: the two experts of a row differ; within the rows of one device no expert is named by more than 5 rows. `ids_backward`: the two experts of a row differ; within the rows of one device no expert is named by more than 5 rows.
All inputs are finite; a program needn't handle non-finite values.
Results may differ from a plain program's by a relative error of at most 0.013.
Values may be sent and summed in bfloat16 or wider, within the bound.
A program may use at most 128 MiB of HBM per device.

v0:
```python
import functools

import jax
import jax.numpy as jnp
from jax import lax
from jax.experimental import pallas as pl
from jax.experimental.pallas import tpu as pltpu
from jax.sharding import PartitionSpec as P

GROUP = 16
CAP = 5


def shifted(block, axis, distance):
    devices = range(lax.axis_size(axis))
    route = [(i - distance, i) for i in devices if i - distance in devices]
    return lax.ppermute(block, axis, route)


def slot_tables(expert_ids, gate_values, experts):
    row_count = expert_ids.shape[0]
    flat_ids = expert_ids.reshape(row_count * 2)
    window = jnp.arange(experts, dtype=jnp.int32)
    member = (flat_ids[None, :] == window[:, None]).astype(jnp.int32)
    before = jnp.cumsum(member, axis=1, dtype=jnp.int32) - member
    positions = jnp.arange(CAP, dtype=jnp.int32)
    picked_slots = (
        member[:, None, :] * (before[:, None, :] == positions[None, :, None]).astype(jnp.int32)
    ).astype(jnp.float32)
    picked_slots = picked_slots.reshape(experts * CAP, row_count, 2)
    select = jnp.sum(picked_slots, axis=2)
    weighted = jnp.sum(picked_slots * gate_values[None, :, :], axis=2)
    return (select, weighted)


def pack_direct(stacked, groups):
    stacks = stacked.shape[0]
    feature_width = stacked.shape[2]
    shaped = stacked.reshape(stacks, groups, 1, CAP, feature_width)
    spread_out = jnp.broadcast_to(shaped, (stacks, groups, GROUP, CAP, feature_width))
    return spread_out.reshape(stacks, groups * GROUP, CAP, feature_width)


def expert_forward(arriving, local_in, local_out):
    feature_width = arriving.shape[-1]
    preact = jnp.dot(
        arriving.reshape(-1, feature_width), local_in, preferred_element_type=jnp.float32
    )
    hidden = jax.nn.silu(preact).astype(jnp.bfloat16)
    partial_out = jnp.dot(hidden, local_out, preferred_element_type=jnp.float32).astype(
        jnp.bfloat16
    )
    return partial_out.reshape(arriving.shape)


def expert_backward(row_part, grad_part, local_in, local_out):
    feature_width = row_part.shape[-1]
    preact = jnp.dot(
        row_part.reshape(-1, feature_width), local_in, preferred_element_type=jnp.float32
    )
    sigmoid_v = jax.nn.sigmoid(preact)
    slope_v = sigmoid_v * (1.0 + preact * (1.0 - sigmoid_v))
    grad_hidden = jnp.einsum(
        "rd,hd->rh",
        grad_part.reshape(-1, feature_width),
        local_out,
        preferred_element_type=jnp.float32,
    )
    grad_pre = (grad_hidden * slope_v).astype(jnp.bfloat16)
    partial_grad = jnp.einsum(
        "rh,dh->rd", grad_pre, local_in, preferred_element_type=jnp.float32
    ).astype(jnp.bfloat16)
    return partial_grad.reshape(row_part.shape)


def gather_groups(returned, groups):
    feature_width = returned.shape[-1]
    summed = jnp.sum(
        returned.reshape(groups, GROUP, CAP, feature_width).astype(jnp.float32), axis=1
    )
    return summed.reshape(groups * CAP, feature_width)


def per_device(
    handoff,
    saved_inputs,
    cotangent,
    ids_forward,
    gates_forward,
    ids_backward,
    gates_backward,
    weight_in,
    weight_out,
):
    highest = lax.Precision.HIGHEST
    groups = lax.axis_size("expert") // GROUP
    segment_index = lax.axis_index("segment")
    last_segment = lax.axis_size("segment") - 1
    arrived = shifted(handoff, "segment", 1)
    inputs = jnp.where(segment_index == 0, handoff, arrived)[0]
    returned = shifted(cotangent, "segment", -1)
    upstream = jnp.where(segment_index == last_segment, cotangent, returned)[0]
    local_in = weight_in[0]
    local_out = weight_out[0]
    select_f, weigh_f = slot_tables(ids_forward[0], gates_forward[0], groups)
    picked = jnp.dot(
        select_f.astype(jnp.bfloat16), inputs, preferred_element_type=jnp.float32
    ).astype(jnp.bfloat16)
    select_b, weigh_b = slot_tables(ids_backward[0], gates_backward[0], groups)
    rows_back = jnp.dot(
        select_b.astype(jnp.bfloat16), saved_inputs[0], preferred_element_type=jnp.float32
    ).astype(jnp.bfloat16)
    grads_out = jnp.dot(
        weigh_b, upstream.astype(jnp.float32), precision=highest, preferred_element_type=jnp.float32
    ).astype(jnp.bfloat16)
    backward_stack = jnp.stack([rows_back, grads_out])
    arriving_f = lax.all_to_all(
        pack_direct(picked[None], groups), "expert", split_axis=1, concat_axis=1, tiled=True
    )
    arriving_b = lax.all_to_all(
        pack_direct(backward_stack, groups), "expert", split_axis=1, concat_axis=1, tiled=True
    )
    partial_f = expert_forward(arriving_f[0], local_in, local_out)
    back_f = lax.all_to_all(partial_f, "expert", split_axis=0, concat_axis=0, tiled=True)
    combined = gather_groups(back_f, groups)
    expert_mix = jnp.dot(
        weigh_f.T, combined, precision=highest, preferred_element_type=jnp.float32
    ).astype(jnp.bfloat16)
    partial_b = expert_backward(arriving_b[0], arriving_b[1], local_in, local_out)
    back_b = lax.all_to_all(partial_b, "expert", split_axis=0, concat_axis=0, tiled=True)
    slot_grads = gather_groups(back_b, groups)
    input_grads = jnp.dot(
        select_b.T, slot_grads, precision=highest, preferred_element_type=jnp.float32
    ).astype(jnp.bfloat16)
    return (expert_mix[None], input_grads[None])


MESH = pl.DeviceIdType.MESH
BLOCK = 16
HALF = 8
PARTS = 2
LANES = 128


def flipped(position, mask):
    bit = 1
    while bit <= mask:
        if mask & bit:
            position = position + bit * (1 - 2 * ((position // bit) % 2))
        bit *= 2
    return position


def exchange_kernel(
    planes,
    wire,
    ids_f_hbm,
    gates_f_hbm,
    ids_b_hbm,
    gates_b_hbm,
    handoff,
    saved,
    cotangent,
    weight_in,
    weight_out,
    out_f,
    out_b,
    rows_x,
    rows_s,
    w_in_side,
    w_out_side,
    blocks,
    req_send,
    req_recv,
    resp_send,
    resp_recv,
    own_rows,
    pair_send,
    pair_keep,
    pair_recv,
    y_send,
    y_keep,
    y_recv,
    z_send,
    z_recv,
    own_sum,
    ids_f,
    gates_f,
    ids_b,
    gates_b,
    scatter,
    gate_wide,
    local_sem,
    send_sem,
    recv_sem,
):
    segment = lax.axis_index("segment")
    expert = lax.axis_index("expert")
    row_count, width = rows_x.shape
    tail_width = width - wire
    hidden = weight_out.shape[0]

    def at_expert(mask):
        return {"expert": flipped(expert, mask)}

    other_segment = {"segment": 1 - segment}
    sibling = at_expert(1)
    across = at_expert(2)
    mates = [None] + [at_expert(4 * k) for k in range(1, planes)]

    barrier = pltpu.get_barrier_semaphore()
    partners = [other_segment, sibling, across] + mates[1:]
    for partner in partners:
        pl.semaphore_signal(barrier, inc=1, device_id=partner, device_id_type=MESH)

    tables = [
        pltpu.make_async_copy(source, target, local_sem.at[4 + i])
        for i, (source, target) in enumerate(
            [(ids_f_hbm, ids_f), (gates_f_hbm, gates_f), (ids_b_hbm, ids_b), (gates_b_hbm, gates_b)]
        )
    ]
    for table_copy in tables:
        table_copy.start()

    @pl.when(segment == 0)
    def _():
        pltpu.make_async_copy(handoff, rows_x, local_sem.at[0]).start()

    @pl.when(segment != 0)
    def _():
        pltpu.make_async_copy(cotangent, rows_x, local_sem.at[0]).start()

    load_x = pltpu.make_async_copy(handoff, rows_x, local_sem.at[0])
    load_s = pltpu.make_async_copy(saved, rows_s, local_sem.at[1])
    load_in = pltpu.make_async_copy(weight_in, w_in_side.at[:, 0:hidden], local_sem.at[2])
    load_out = pltpu.make_async_copy(weight_out, w_out_side.at[0:hidden, :], local_sem.at[3])
    load_s.start()
    load_in.start()
    load_out.start()

    count = [0]
    started = []

    def remote(source, target, device):
        number = count[0]
        count[0] += 1
        return pltpu.make_async_remote_copy(
            src_ref=source,
            dst_ref=target,
            send_sem=send_sem.at[number],
            recv_sem=recv_sem.at[number],
            device_id=device,
            device_id_type=MESH,
        )

    def begin(copy):
        copy.start()
        started.append(copy)

    request = remote(req_send, req_recv, other_segment)
    response = remote(resp_send, resp_recv, other_segment)

    def cuts(total):
        tiles = total // LANES
        edges = [tiles * i // PARTS * LANES for i in range(PARTS + 1)]
        return [slice(low, high) for low, high in zip(edges[:-1], edges[1:])]

    wide_cuts, wire_cuts = cuts(width), cuts(wire)

    def gather(source, target, device):
        return [
            remote(blocks.at[(*source, slice(None), cut)], blocks.at[(*target, slice(None), cut)], device)
            for cut in wide_cuts
        ]

    gather_z = [None] + [gather((0, 0, 0), (k, 0, 0), mates[k]) for k in range(1, planes)]
    gather_y = [gather((k, 0, 0), (k, 1, 0), across) for k in range(planes)]
    gather_c0 = [gather((k, 0, 0), (k, 0, 1), sibling) for k in range(planes)]
    gather_c1 = [gather((k, 1, 0), (k, 1, 1), sibling) for k in range(planes)]
    reduce_c = [
        [remote(pair_send.at[k, :, :, cut], pair_recv.at[k, :, :, cut], sibling) for cut in wire_cuts]
        for k in range(planes)
    ]
    reduce_y = [
        [remote(y_send.at[k, :, cut], y_recv.at[k, :, cut], across) for cut in wire_cuts]
        for k in range(planes)
    ]
    reduce_z = [None] + [
        [remote(z_send.at[k, :, cut], z_recv.at[k, :, cut], mates[k]) for cut in wire_cuts]
        for k in range(1, planes)
    ]

    for table_copy in tables:
        table_copy.wait()
    earlier = jnp.where(
        lax.broadcasted_iota(jnp.int32, (row_count, row_count), 0)
        < lax.broadcasted_iota(jnp.int32, (row_count, row_count), 1),
        1.0,
        0.0,
    ).astype(jnp.bfloat16)

    def ranks(ids, gates):
        first, second = ids[0:1, :] == 0, ids[1:2, :] == 0
        member = jnp.where(first | second, 1.0, 0.0)
        gate = jnp.where(first, gates[0:1, :], 0.0) + jnp.where(second, gates[1:2, :], 0.0)
        wide = jnp.broadcast_to(member, (BLOCK, row_count))
        rank = jnp.dot(wide.astype(jnp.bfloat16), earlier, preferred_element_type=jnp.float32)
        return wide, rank.astype(jnp.int32), gate

    slot_row = lax.broadcasted_iota(jnp.int32, (BLOCK, row_count), 0)

    def placed(member, rank, offset):
        slot = slot_row - offset
        fits = (slot == rank) & (slot < CAP) & (slot >= 0)
        return jnp.where(fits, member, 0.0)

    member_f, rank_f, gate_f = ranks(ids_f, gates_f)
    member_b, rank_b, gate_b = ranks(ids_b, gates_b)
    later = (segment * jnp.ones((), jnp.int32)).astype(jnp.float32)
    first_f, first_b = placed(member_f, rank_f, 0), placed(member_b, rank_b, 0) * gate_b
    last_f, last_b = placed(member_f, rank_f, 2 * CAP), placed(member_b, rank_b, 2 * CAP) * gate_b
    asked = (first_b * (1.0 - later) + first_f * later)[0:HALF]
    mine = last_f * (1.0 - later) + last_b * later
    kept = placed(member_b, rank_b, CAP)
    req_send[...] = jnp.concatenate([asked, jnp.zeros((HALF, LANES - row_count), jnp.float32)], axis=1)
    pl.semaphore_wait(barrier, len(partners))
    begin(request)

    def picked(weights, rows_ref):
        scale = jnp.sum(weights, axis=1, keepdims=True)
        choose = jnp.where(weights != 0.0, 1.0, 0.0).astype(jnp.bfloat16)
        return jnp.dot(choose, rows_ref[...], preferred_element_type=jnp.float32) * scale

    load_x.wait()
    load_s.wait()
    own_rows[...] = picked(mine, rows_x) + picked(kept, rows_s)
    request.wait_recv()
    resp_send[...] = picked(req_recv[:, 0:row_count], rows_x).astype(jnp.bfloat16)
    begin(response)
    load_in.wait()
    load_out.wait()
    turn = 512 if width % 512 == 0 else LANES

    def transposes(step, carry):
        piece = pl.ds(pl.multiple_of(step * turn, turn), turn)
        w_in_side[piece, hidden : 2 * hidden] = w_out_side[0:hidden, piece].T
        w_out_side[hidden : 2 * hidden, piece] = w_in_side[piece, 0:hidden].T
        return carry

    lax.fori_loop(0, width // turn, transposes, 0)
    unit = jnp.where(
        lax.broadcasted_iota(jnp.int32, (row_count, row_count), 0)
        == lax.broadcasted_iota(jnp.int32, (row_count, row_count), 1),
        1.0,
        0.0,
    )
    by_row = (((1,), (1,)), ((), ()))
    for i, (member, rank, offset) in enumerate(
        [(member_f, rank_f, 0), (member_b, rank_b, CAP), (member_f, rank_f, 2 * CAP), (member_b, rank_b, 2 * CAP)]
    ):
        ones = placed(member, rank, offset)
        scatter[i] = lax.dot_general(
            unit.astype(jnp.bfloat16),
            jnp.concatenate([ones, ones], axis=0).astype(jnp.bfloat16),
            by_row,
            preferred_element_type=jnp.float32,
        ).astype(jnp.bfloat16)
    gate_wide[...] = lax.dot_general(
        unit,
        jnp.broadcast_to(gate_f, (LANES, row_count)),
        by_row,
        precision=lax.Precision.HIGHEST,
        preferred_element_type=jnp.float32,
    )
    response.wait_recv()
    own_rows[0:HALF, :] = own_rows[0:HALF, :] + resp_recv[...].astype(jnp.float32)
    blocks[0, 0, 0] = own_rows[...].astype(jnp.bfloat16)

    def spread(k):
        for part in range(PARTS):
            if k > 0:
                gather_z[k][part].wait_recv()
            begin(gather_y[k][part])
            begin(gather_c0[k][part])

    def relay(k):
        for part in range(PARTS):
            gather_y[k][part].wait_recv()
            begin(gather_c1[k][part])

    batch = 4 * BLOCK
    place = lax.broadcasted_iota(jnp.int32, (batch, hidden), 0) % BLOCK
    chunk = 256 if tail_width % 256 == 0 and wire % 256 == 0 else LANES

    def compute(k):
        for part in range(PARTS):
            gather_c0[k][part].wait_recv()
            gather_c1[k][part].wait_recv()

        def contract(step, total):
            piece = pl.ds(pl.multiple_of(step * turn, turn), turn)
            return total + jnp.dot(
                blocks[k, :, :, :, piece].reshape(batch, turn),
                w_in_side[piece, :],
                preferred_element_type=jnp.float32,
            )

        both = lax.fori_loop(
            0, width // turn, contract, jnp.zeros((batch, 2 * hidden), jnp.float32), unroll=True
        )
        pre = both[:, 0:hidden]
        grad_hidden = both[:, hidden:]
        grad_hidden = (
            pltpu.roll(grad_hidden, CAP, 0) * (1.0 - later) + pltpu.roll(grad_hidden, batch - CAP, 0) * later
        )
        gate = 1.0 / (1.0 + jnp.exp(-pre))
        silu = pre * gate
        silu = pltpu.roll(silu, batch - 2 * CAP, 0) * (1.0 - later) + silu * later
        forward = jnp.where(place < CAP, silu, 0.0)
        slope = gate * (1.0 + pre * (1.0 - gate))
        backward = jnp.where((place >= CAP) & (place < 2 * CAP), grad_hidden * slope, 0.0)
        late_f = pltpu.roll(forward, 2 * CAP, 0).astype(jnp.bfloat16)
        late_b = pltpu.roll(backward, CAP, 0).astype(jnp.bfloat16)
        main = jnp.concatenate([forward, backward], axis=1).astype(jnp.bfloat16)

        def put(start, value):
            columns = pl.ds(start, chunk)
            value = value.reshape(2, 2, BLOCK, chunk)
            pair_keep[k, :, :, columns] = value[:, 0]
            pair_send[k, :, :, columns] = value[:, 1].astype(jnp.bfloat16)

        def product(start):
            return jnp.dot(main, w_out_side[:, pl.ds(start, chunk)], preferred_element_type=jnp.float32)

        def pieces(step, carry):
            start = pl.multiple_of(step * chunk, chunk)
            late = pl.ds(pl.multiple_of(wire + step * chunk, chunk), chunk)
            put(
                start,
                product(start)
                + jnp.dot(late_f, w_out_side[0:hidden, late], preferred_element_type=jnp.float32),
            )
            start = pl.multiple_of(tail_width + step * chunk, chunk)
            put(
                start,
                product(start)
                + jnp.dot(
                    late_b, w_out_side[hidden : 2 * hidden, late], preferred_element_type=jnp.float32
                ),
            )
            return carry

        lax.fori_loop(0, tail_width // chunk, pieces, 0, unroll=True)
        for start in range(2 * tail_width, wire, chunk):
            put(start, product(start))
        for copy in reduce_c[k]:
            begin(copy)

    def join_pair(k):
        for part, cut in enumerate(wire_cuts):
            reduce_c[k][part].wait_recv()
            sent = pair_keep[k, 1, :, cut] + pair_recv[k, 1, :, cut].astype(jnp.float32)
            y_send[k, :, cut] = sent.astype(jnp.bfloat16)
            begin(reduce_y[k][part])
            y_keep[k, :, cut] = pair_keep[k, 0, :, cut] + pair_recv[k, 0, :, cut].astype(jnp.float32)

    def join_plane(k):
        for part, cut in enumerate(wire_cuts):
            reduce_y[k][part].wait_recv()
            total = y_keep[k, :, cut] + y_recv[k, :, cut].astype(jnp.float32)
            if k == 0:
                own_sum[:, cut] = total
            else:
                z_send[k, :, cut] = total.astype(jnp.bfloat16)
                begin(reduce_z[k][part])

    for k in range(1, planes):
        for copy in gather_z[k]:
            begin(copy)
    spread(0)
    last = planes - 1
    for step in range(last):
        spread(step + 1)
        if step == last - 1:
            for k in range(step):
                join_pair(k)
        relay(step)
        compute(step)
    join_pair(last - 1)
    relay(last)
    join_plane(0)
    compute(last)
    join_pair(last)
    for k in range(1, planes):
        join_plane(k)

    heads = scatter[0:2].reshape(2 * row_count, 2 * BLOCK)
    late_rows_f, late_rows_b = scatter[2], scatter[3]
    wide_gate = jnp.concatenate([gate_wide[...]] * (chunk // LANES), axis=1)
    for k in range(1, planes):
        for copy in reduce_z[k]:
            copy.wait_recv()

    def halves(start):
        columns = slice(start, start + chunk)
        total = own_sum[:, columns]
        for k in range(1, planes):
            total = total + z_recv[k, :, columns].astype(jnp.float32)
        high = total.astype(jnp.bfloat16)
        low = (total - high.astype(jnp.float32)).astype(jnp.bfloat16)
        return jnp.concatenate([high, low], axis=0)

    for start in range(0, wire, chunk):
        both = halves(start)
        value = jnp.dot(heads, both, preferred_element_type=jnp.float32)
        out_f[:, start : start + chunk] = (value[0:row_count] * wide_gate).astype(jnp.bfloat16)
        out_b[:, start : start + chunk] = value[row_count:].astype(jnp.bfloat16)
        if start < tail_width:
            value = jnp.dot(late_rows_f, both, preferred_element_type=jnp.float32) * wide_gate
            out_f[:, wire + start : wire + start + chunk] = value.astype(jnp.bfloat16)
        elif start < 2 * tail_width:
            late = wire + start - tail_width
            value = jnp.dot(late_rows_b, both, preferred_element_type=jnp.float32)
            out_b[:, late : late + chunk] = value.astype(jnp.bfloat16)
    for copy in started:
        copy.wait_send()


def exchange(planes, handoff, saved_inputs, cotangent, ids_forward, gates_forward, ids_backward, gates_backward, weight_in, weight_out):
    rows, width = handoff.shape[1:]
    hidden = weight_out.shape[1]
    tiles = width // LANES
    wire = -(-2 * tiles // 3) * LANES
    bf16, f32 = jnp.bfloat16, jnp.float32
    copies = 2 + PARTS * (2 * (planes - 1) + 5 * planes)
    vmem = pl.BlockSpec(memory_space=pltpu.VMEM)
    hbm = pl.BlockSpec(memory_space=pl.ANY)
    mixed, grads = pl.pallas_call(
        functools.partial(exchange_kernel, planes, wire),
        out_shape=[jax.ShapeDtypeStruct((rows, width), bf16)] * 2,
        in_specs=[hbm] * 9,
        out_specs=[vmem] * 2,
        scratch_shapes=[
            pltpu.VMEM((rows, width), bf16),
            pltpu.VMEM((rows, width), bf16),
            pltpu.VMEM((width, 2 * hidden), bf16),
            pltpu.VMEM((2 * hidden, width), bf16),
            pltpu.VMEM((planes, 2, 2, BLOCK, width), bf16),
            pltpu.VMEM((HALF, LANES), f32),
            pltpu.VMEM((HALF, LANES), f32),
            pltpu.VMEM((HALF, width), bf16),
            pltpu.VMEM((HALF, width), bf16),
            pltpu.VMEM((BLOCK, width), f32),
            pltpu.VMEM((planes, 2, BLOCK, wire), bf16),
            pltpu.VMEM((planes, 2, BLOCK, wire), f32),
            pltpu.VMEM((planes, 2, BLOCK, wire), bf16),
            pltpu.VMEM((planes, BLOCK, wire), bf16),
            pltpu.VMEM((planes, BLOCK, wire), f32),
            pltpu.VMEM((planes, BLOCK, wire), bf16),
            pltpu.VMEM((planes, BLOCK, wire), bf16),
            pltpu.VMEM((planes, BLOCK, wire), bf16),
            pltpu.VMEM((BLOCK, wire), f32),
            pltpu.VMEM((2, rows), jnp.int32),
            pltpu.VMEM((2, rows), f32),
            pltpu.VMEM((2, rows), jnp.int32),
            pltpu.VMEM((2, rows), f32),
            pltpu.VMEM((4, rows, 2 * BLOCK), bf16),
            pltpu.VMEM((rows, LANES), f32),
            pltpu.SemaphoreType.DMA((8,)),
            pltpu.SemaphoreType.DMA((copies,)),
            pltpu.SemaphoreType.DMA((copies,)),
        ],
        compiler_params=pltpu.CompilerParams(
            collective_id=0, has_side_effects=True
        ),
    )(
        ids_forward[0].T,
        gates_forward[0].T,
        ids_backward[0].T,
        gates_backward[0].T,
        handoff[0],
        saved_inputs[0],
        cotangent[0],
        weight_in[0],
        weight_out[0],
    )
    return (mixed[None], grads[None])


def device_body(mesh):
    segments, experts = mesh.shape["segment"], mesh.shape["expert"]
    planes = experts // 4
    if segments == 2 and experts == GROUP and planes & (planes - 1) == 0:
        return functools.partial(exchange, planes)
    return per_device


def solution(mesh):
    return jax.shard_map(
        device_body(mesh),
        mesh=mesh,
        in_specs=(
            P("segment", "expert", None),
            P("segment", "expert", None),
            P("segment", "expert", None),
            P("segment", "expert", None),
            P("segment", "expert", None),
            P("segment", "expert", None),
            P("segment", "expert", None),
            P("segment", None, "expert"),
            P("segment", "expert", None),
        ),
        out_specs=(P("segment", "expert", None), P("segment", "expert", None)),
        check_vma=False,
    )
```

profile of v0, /device:TPU:0, one launch (start us, length us, event | category | flops | bytes accessed | tf_op | source)
XLA Modules:
  0.0 47.0 jit_solution(2262054048768695469)
XLA Ops:
  0.6 43.7 %shard_map.104 = (bf16[64,4096]{1,0:T(8,128)(2,1)}, bf16[64,4096]{1,0:T(8,128)(2,1)}) custom-call(s32[2,64]{1,0:T(2,128)} %bitcast.26, f32[2,64]{1,0:T(2,128)} %bitcast.27, s32[2,64]{1,0:T(2,128)} %bitcast.28, f32[2,64]{1,0:T(2,128)} %bitcast.29, bf16[64,4096]{1,0:T(8,128)(2,1)} %bitcast.23, bf16[64,4096]{1,0:T(8,128)(2,1)} %bitcast.24, ...), custom_call_target="tpu_custom_call" | custom-call | tf_op jit(solution)/shard_map/pallas_call | solution.py:538
  44.3 0.0 copy-start
  44.3 1.9 %copy.13 = bf16[1,64,4096]{2,1,0:T(8,128)(2,1)} copy(bf16[1,64,4096]{2,1,0:T(8,128)(2,1)} %bitcast.22) | data formatting | bytes 1048576
  46.2 0.0 copy-done
  46.2 0.8 %copy.14 = bf16[1,64,4096]{2,1,0:T(8,128)(2,1)} copy(bf16[1,64,4096]{2,1,0:T(8,128)(2,1)S(1)} %bitcast.21) | data formatting | bytes 1048576
Async XLA Ops:
  44.3 1.9 %copy-start = (bf16[64,4096]{1,0:T(8,128)(2,1)S(1)}, bf16[64,4096]{1,0:T(8,128)(2,1)}, u32[]{:S(2)}) copy-start(bf16[64,4096]{1,0:T(8,128)(2,1)} %get-tuple-element.5) | copy-start | bytes 1572868
where the time goes:
time: 47.2 us; the launch traced here: 47 us
  Pallas kernels  43.7 us (93%)
  local copies, waits for them, and re-layouts  2.72 us (6%)
  between operations  0.65 us (1%)
    pallas_call x1, Pallas kernels, exchange(): pl.pallas_call(functools.partial(exchange_kernel, planes, wire), out_shap...  43.7 us
    unnamed x4, local copies, waits for them, and re-layouts  2.72 us

commit v1 on v0

v1 whole, which is shorter than its diff:
```python
import functools

import jax
import jax.numpy as jnp
from jax import lax
from jax.experimental import pallas as pl
from jax.experimental.pallas import tpu as pltpu
from jax.sharding import PartitionSpec as P

GROUP = 16
CAP = 5


def shifted(block, axis, distance):
    devices = range(lax.axis_size(axis))
    route = [(i - distance, i) for i in devices if i - distance in devices]
    return lax.ppermute(block, axis, route)


def slot_tables(expert_ids, gate_values, experts):
    row_count = expert_ids.shape[0]
    flat_ids = expert_ids.reshape(row_count * 2)
    window = jnp.arange(experts, dtype=jnp.int32)
    member = (flat_ids[None, :] == window[:, None]).astype(jnp.int32)
    before = jnp.cumsum(member, axis=1, dtype=jnp.int32) - member
    positions = jnp.arange(CAP, dtype=jnp.int32)
    picked_slots = (
        member[:, None, :] * (before[:, None, :] == positions[None, :, None]).astype(jnp.int32)
    ).astype(jnp.float32)
    picked_slots = picked_slots.reshape(experts * CAP, row_count, 2)
    select = jnp.sum(picked_slots, axis=2)
    weighted = jnp.sum(picked_slots * gate_values[None, :, :], axis=2)
    return (select, weighted)


def pack_direct(stacked, groups):
    stacks = stacked.shape[0]
    feature_width = stacked.shape[2]
    shaped = stacked.reshape(stacks, groups, 1, CAP, feature_width)
    spread_out = jnp.broadcast_to(shaped, (stacks, groups, GROUP, CAP, feature_width))
    return spread_out.reshape(stacks, groups * GROUP, CAP, feature_width)


def expert_forward(arriving, local_in, local_out):
    feature_width = arriving.shape[-1]
    preact = jnp.dot(
        arriving.reshape(-1, feature_width), local_in, preferred_element_type=jnp.float32
    )
    hidden = jax.nn.silu(preact).astype(jnp.bfloat16)
    partial_out = jnp.dot(hidden, local_out, preferred_element_type=jnp.float32).astype(
        jnp.bfloat16
    )
    return partial_out.reshape(arriving.shape)


def expert_backward(row_part, grad_part, local_in, local_out):
    feature_width = row_part.shape[-1]
    preact = jnp.dot(
        row_part.reshape(-1, feature_width), local_in, preferred_element_type=jnp.float32
    )
    sigmoid_v = jax.nn.sigmoid(preact)
    slope_v = sigmoid_v * (1.0 + preact * (1.0 - sigmoid_v))
    grad_hidden = jnp.einsum(
        "rd,hd->rh",
        grad_part.reshape(-1, feature_width),
        local_out,
        preferred_element_type=jnp.float32,
    )
    grad_pre = (grad_hidden * slope_v).astype(jnp.bfloat16)
    partial_grad = jnp.einsum(
        "rh,dh->rd", grad_pre, local_in, preferred_element_type=jnp.float32
    ).astype(jnp.bfloat16)
    return partial_grad.reshape(row_part.shape)


def gather_groups(returned, groups):
    feature_width = returned.shape[-1]
    summed = jnp.sum(
        returned.reshape(groups, GROUP, CAP, feature_width).astype(jnp.float32), axis=1
    )
    return summed.reshape(groups * CAP, feature_width)


def per_device(
    handoff,
    saved_inputs,
    cotangent,
    ids_forward,
    gates_forward,
    ids_backward,
    gates_backward,
    weight_in,
    weight_out,
):
    highest = lax.Precision.HIGHEST
    groups = lax.axis_size("expert") // GROUP
    segment_index = lax.axis_index("segment")
    last_segment = lax.axis_size("segment") - 1
    arrived = shifted(handoff, "segment", 1)
    inputs = jnp.where(segment_index == 0, handoff, arrived)[0]
    returned = shifted(cotangent, "segment", -1)
    upstream = jnp.where(segment_index == last_segment, cotangent, returned)[0]
    local_in = weight_in[0]
    local_out = weight_out[0]
    select_f, weigh_f = slot_tables(ids_forward[0], gates_forward[0], groups)
    picked = jnp.dot(
        select_f.astype(jnp.bfloat16), inputs, preferred_element_type=jnp.float32
    ).astype(jnp.bfloat16)
    select_b, weigh_b = slot_tables(ids_backward[0], gates_backward[0], groups)
    rows_back = jnp.dot(
        select_b.astype(jnp.bfloat16), saved_inputs[0], preferred_element_type=jnp.float32
    ).astype(jnp.bfloat16)
    grads_out = jnp.dot(
        weigh_b, upstream.astype(jnp.float32), precision=highest, preferred_element_type=jnp.float32
    ).astype(jnp.bfloat16)
    backward_stack = jnp.stack([rows_back, grads_out])
    arriving_f = lax.all_to_all(
        pack_direct(picked[None], groups), "expert", split_axis=1, concat_axis=1, tiled=True
    )
    arriving_b = lax.all_to_all(
        pack_direct(backward_stack, groups), "expert", split_axis=1, concat_axis=1, tiled=True
    )
    partial_f = expert_forward(arriving_f[0], local_in, local_out)
    back_f = lax.all_to_all(partial_f, "expert", split_axis=0, concat_axis=0, tiled=True)
    combined = gather_groups(back_f, groups)
    expert_mix = jnp.dot(
        weigh_f.T, combined, precision=highest, preferred_element_type=jnp.float32
    ).astype(jnp.bfloat16)
    partial_b = expert_backward(arriving_b[0], arriving_b[1], local_in, local_out)
    back_b = lax.all_to_all(partial_b, "expert", split_axis=0, concat_axis=0, tiled=True)
    slot_grads = gather_groups(back_b, groups)
    input_grads = jnp.dot(
        select_b.T, slot_grads, precision=highest, preferred_element_type=jnp.float32
    ).astype(jnp.bfloat16)
    return (expert_mix[None], input_grads[None])


MESH = pl.DeviceIdType.MESH
BLOCK = 16
THIRDS = 3
PARTS = 2
LANES = 128


def flipped(position, mask):
    bit = 1
    while bit <= mask:
        if mask & bit:
            position = position + bit * (1 - 2 * ((position // bit) % 2))
        bit *= 2
    return position


def exchange_kernel(
    planes,
    chunk,
    ids_f_hbm,
    gates_f_hbm,
    ids_b_hbm,
    gates_b_hbm,
    handoff,
    saved,
    cotangent,
    weight_in,
    weight_out,
    sums,
    places,
    gate_wide,
    rows_x,
    rows_s,
    w_first,
    w_second,
    blocks,
    req_send,
    req_recv,
    late_send,
    slope,
    y_send,
    y_keep,
    y_recv,
    z_send,
    z_recv,
    own_sum,
    ids_f,
    gates_f,
    ids_b,
    gates_b,
    local_sem,
    send_sem,
    recv_sem,
):
    segment = lax.axis_index("segment")
    expert = lax.axis_index("expert")
    row_count, width = rows_x.shape
    hidden = weight_out.shape[0]
    lengths = [min(chunk, width - q * chunk) for q in range(THIRDS)]

    def at_expert(mask):
        return {"expert": flipped(expert, mask)}

    def at_other(k):
        return {"segment": 1 - segment, "expert": flipped(expert, 4 * k)}

    sibling = at_expert(1)
    across = at_expert(2)
    mates = [None] + [at_expert(4 * k) for k in range(1, planes)]
    others = [at_other(k) for k in range(planes)]

    barrier = pltpu.get_barrier_semaphore()
    partners = mates[1:] + others + [across, sibling]
    for partner in partners:
        pl.semaphore_signal(barrier, inc=1, device_id=partner, device_id_type=MESH)

    tables = [
        pltpu.make_async_copy(source, target, local_sem.at[4 + i])
        for i, (source, target) in enumerate(
            [(ids_f_hbm, ids_f), (gates_f_hbm, gates_f), (ids_b_hbm, ids_b), (gates_b_hbm, gates_b)]
        )
    ]
    for table_copy in tables:
        table_copy.start()

    @pl.when(segment == 0)
    def _():
        pltpu.make_async_copy(handoff, rows_x, local_sem.at[0]).start()

    @pl.when(segment != 0)
    def _():
        pltpu.make_async_copy(cotangent, rows_x, local_sem.at[0]).start()

    load_x = pltpu.make_async_copy(handoff, rows_x, local_sem.at[0])
    load_s = pltpu.make_async_copy(saved, rows_s, local_sem.at[1])
    load_in = pltpu.make_async_copy(weight_in, w_first.at[0, :, 0:hidden], local_sem.at[2])
    load_out = pltpu.make_async_copy(weight_out, w_second.at[0, 0:hidden, :], local_sem.at[3])
    load_s.start()
    load_in.start()
    load_out.start()

    count = [0]
    started = []

    def remote(source, target, device):
        number = count[0]
        count[0] += 1
        return pltpu.make_async_remote_copy(
            src_ref=source,
            dst_ref=target,
            send_sem=send_sem.at[number],
            recv_sem=recv_sem.at[number],
            device_id=device,
            device_id_type=MESH,
        )

    def begin(copy):
        copy.start()
        started.append(copy)

    tiles = chunk // LANES
    edges = [tiles * i // PARTS * LANES for i in range(PARTS + 1)]
    parts = range(PARTS)
    cuts = [slice(low, high) for low, high in zip(edges[:-1], edges[1:])]

    def pieces(part):
        low, high = edges[part], edges[part + 1]
        middle = min(max(lengths[-1], low), high)
        return [
            (start, stop, THIRDS if stop <= lengths[-1] else THIRDS - 1)
            for start, stop in ((low, middle), (middle, high))
            if start < stop
        ]

    request = remote(req_send, req_recv, others[0])
    give_in = remote(weight_in, w_first.at[0, :, hidden : 2 * hidden], sibling)
    give_out = remote(weight_out, w_second.at[0, hidden : 2 * hidden, :], sibling)

    def ship(source, target, device):
        return [remote(source.at[:, cut], target.at[:, cut], device) for cut in cuts]

    gather_z = [
        [None] + [ship(blocks.at[kind, 0], blocks.at[kind, 2 * k], mates[k]) for k in range(1, planes)]
        for kind in range(2)
    ]
    gather_z.append([ship(late_send, blocks.at[2, 2 * k], others[k]) for k in range(planes)])
    gather_y = [
        [ship(blocks.at[kind, 2 * k], blocks.at[kind, 2 * k + 1], across) for k in range(planes)]
        for kind in range(3)
    ]
    reduce_y = [
        [ship(y_send.at[o, k], y_recv.at[o, k], across) for k in range(planes)] for o in range(2)
    ]
    reduce_z = [
        [None] + [ship(z_send.at[o, k], z_recv.at[o, k], mates[k]) for k in range(1, planes)]
        for o in range(2)
    ]

    for table_copy in tables:
        table_copy.wait()
    earlier = jnp.where(
        lax.broadcasted_iota(jnp.int32, (row_count, row_count), 0)
        < lax.broadcasted_iota(jnp.int32, (row_count, row_count), 1),
        1.0,
        0.0,
    ).astype(jnp.bfloat16)
    block_row = lax.broadcasted_iota(jnp.int32, (BLOCK, row_count), 0)
    third = sum((block_row >= CAP * q).astype(jnp.int32) for q in range(1, THIRDS + 1))
    slot = block_row - CAP * third

    def ranks(ids, gates):
        first, second = ids[0:1, :] == 0, ids[1:2, :] == 0
        member = jnp.where(first | second, 1.0, 0.0)
        gate = jnp.where(first, gates[0:1, :], 0.0) + jnp.where(second, gates[1:2, :], 0.0)
        wide = jnp.broadcast_to(member, (BLOCK, row_count))
        rank = jnp.dot(wide.astype(jnp.bfloat16), earlier, preferred_element_type=jnp.float32)
        placed = jnp.where((slot == rank.astype(jnp.int32)) & (third < THIRDS), wide, 0.0)
        return placed, gate

    placed_f, gate_f = ranks(ids_f, gates_f)
    placed_b, gate_b = ranks(ids_b, gates_b)
    later = (segment * jnp.ones((), jnp.int32)).astype(jnp.float32)
    scaled_b = placed_b * gate_b
    asked = scaled_b * (1.0 - later) + placed_f * later
    mine = placed_f * (1.0 - later) + scaled_b * later
    req_send[...] = jnp.concatenate([asked, jnp.zeros((BLOCK, LANES - row_count), jnp.float32)], axis=1)
    pl.semaphore_wait(barrier, len(partners))
    begin(request)

    def pick(weights, rows_ref, target):
        scale = jnp.sum(weights, axis=1, keepdims=True)
        choose = [
            jnp.where((weights != 0.0) & (third == q), 1.0, 0.0).astype(jnp.bfloat16) for q in range(THIRDS)
        ]
        for part in parts:
            for start, stop, thirds in pieces(part):
                total = sum(
                    jnp.dot(
                        choose[q],
                        rows_ref[:, q * chunk + start : q * chunk + stop],
                        preferred_element_type=jnp.float32,
                    )
                    for q in range(thirds)
                )
                target[:, start:stop] = (total * scale).astype(jnp.bfloat16)

    load_x.wait()
    pick(mine, rows_x, blocks.at[0, 0])
    for part in parts:
        begin(gather_y[0][0][part])
        for k in range(1, planes):
            begin(gather_z[0][k][part])
    load_s.wait()
    pick(placed_b, rows_s, blocks.at[1, 0])
    for part in parts:
        begin(gather_y[1][0][part])
        for k in range(1, planes):
            begin(gather_z[1][k][part])
    begin(give_in)
    begin(give_out)
    request.wait_recv()
    pick(req_recv[:, 0:row_count], rows_x, late_send)
    for part in parts:
        for k in range(planes):
            begin(gather_z[2][k][part])

    turn = 512 if width % 512 == 0 else LANES

    def transpose(low):
        half = slice(low, low + hidden)

        def step(number, carry):
            piece = pl.ds(pl.multiple_of(number * turn, turn), turn)
            w_first[1, piece, half] = w_second[0, half, piece].T
            w_second[1, half, piece] = w_first[0, piece, half].T
            return carry

        lax.fori_loop(0, width // turn, step, 0)

    def relay(kind, k):
        for part in parts:
            gather_z[kind][k][part].wait_recv()
            begin(gather_y[kind][k][part])

    load_in.wait()
    load_out.wait()
    transpose(0)
    for k in range(1, planes):
        relay(0, k)
    give_in.wait_recv()
    give_out.wait_recv()
    transpose(hidden)
    for k in range(1, planes):
        relay(1, k)
    unit = jnp.where(
        lax.broadcasted_iota(jnp.int32, (row_count, row_count), 0)
        == lax.broadcasted_iota(jnp.int32, (row_count, row_count), 1),
        1.0,
        0.0,
    )
    by_row = (((1,), (1,)), ((), ()))
    for i, placed in enumerate([placed_f, placed_b]):
        places[i] = lax.dot_general(
            unit.astype(jnp.bfloat16),
            placed.astype(jnp.bfloat16),
            by_row,
            preferred_element_type=jnp.float32,
        ).astype(jnp.bfloat16)
    gate_wide[...] = lax.dot_general(
        unit,
        jnp.broadcast_to(gate_f, (LANES, row_count)),
        by_row,
        precision=lax.Precision.HIGHEST,
        preferred_element_type=jnp.float32,
    )

    batch = 2 * planes * BLOCK
    place = lax.broadcasted_iota(jnp.int32, (batch, 2 * hidden), 0) % BLOCK

    def arrived(kind):
        for part in parts:
            for k in range(planes):
                gather_y[kind][k][part].wait_recv()

    def contract(kind, side):
        totals = [
            jnp.dot(
                blocks[kind, :, :, 0 : lengths[q]].reshape(batch, lengths[q]),
                w_first[side, q * chunk : q * chunk + lengths[q], :],
                preferred_element_type=jnp.float32,
            )
            for q in range(THIRDS)
        ]
        value = totals[0]
        for q in range(1, THIRDS):
            value = value + pltpu.roll(totals[q], batch - CAP * q, 0)
        return value

    def sigmoid(value):
        return 1.0 / (1.0 + jnp.exp(-value))

    order = [k for k in range(planes - 1, -1, -1)]

    def expand(value, side, o):
        value = jnp.where(place < CAP, value, 0.0)
        left = [pltpu.roll(value, CAP * q, 0).astype(jnp.bfloat16) if q else value.astype(jnp.bfloat16) for q in range(THIRDS)]
        for part in parts:
            for start, stop, thirds in pieces(part):
                total = sum(
                    jnp.dot(
                        left[q],
                        w_second[side, :, q * chunk + start : q * chunk + stop],
                        preferred_element_type=jnp.float32,
                    )
                    for q in range(thirds)
                ).reshape(planes, 2, BLOCK, stop - start)
                y_keep[o, :, :, start:stop] = total[:, 0]
                y_send[o, :, :, start:stop] = total[:, 1].astype(jnp.bfloat16)
            for k in order:
                begin(reduce_y[o][k][part])

    def join(o, part):
        cut = cuts[part]
        for k in order:
            reduce_y[o][k][part].wait_recv()
            total = y_keep[o, k, :, cut] + y_recv[o, k, :, cut].astype(jnp.float32)
            if k == 0:
                own_sum[o, :, cut] = total
            else:
                z_send[o, k, :, cut] = total.astype(jnp.bfloat16)
                begin(reduce_z[o][k][part])

    relay(2, 0)
    arrived(0)
    first = contract(0, segment)
    relay(2, 1)
    arrived(1)
    pre = contract(1, 0)
    gate = sigmoid(pre)
    slope[...] = gate * (1.0 + pre * (1.0 - gate))
    expand(first * sigmoid(first) * (1.0 - later) + first * slope[...] * later, segment, 0)
    for k in range(2, planes):
        relay(2, k)
    arrived(2)
    last = contract(2, 1 - segment)
    expand(last * slope[...] * (1.0 - later) + last * sigmoid(last) * later, 1 - segment, 1)
    for o in range(2):
        for part in parts:
            join(o, part)
    for o in range(2):
        total = own_sum[o]
        for k in range(1, planes):
            for part in parts:
                reduce_z[o][k][part].wait_recv()
            total = total + z_recv[o, k].astype(jnp.float32)
        sums[segment if o == 0 else 1 - segment] = total.astype(jnp.bfloat16)
    for copy in started:
        copy.wait_send()


def scatter_kernel(chunk, sums, places, gate_wide, out_f, out_b):
    width = out_f.shape[1]
    column = lax.broadcasted_iota(jnp.int32, places.shape[1:], 1)
    gate = gate_wide[:, 0:1]
    for q in range(THIRDS):
        low, high = q * chunk, min((q + 1) * chunk, width)
        inside = (column >= CAP * q) & (column < CAP * (q + 1))
        for i, out in enumerate([out_f, out_b]):
            value = jnp.dot(
                jnp.where(inside, places[i], 0.0).astype(jnp.bfloat16),
                sums[i, :, 0 : high - low],
                preferred_element_type=jnp.float32,
            )
            out[:, low:high] = (value * gate if i == 0 else value).astype(jnp.bfloat16)


def exchange(planes, handoff, saved_inputs, cotangent, ids_forward, gates_forward, ids_backward, gates_backward, weight_in, weight_out):
    rows, width = handoff.shape[1:]
    hidden = weight_out.shape[1]
    chunk = -(-(width // LANES) // THIRDS) * LANES
    bf16, f32 = jnp.bfloat16, jnp.float32
    copies = 3 + PARTS * (2 * (2 * planes - 1) + 2 * planes + 2 * (2 * planes - 1))
    vmem = pl.BlockSpec(memory_space=pltpu.VMEM)
    hbm = pl.BlockSpec(memory_space=pl.ANY)
    sums, places, gate_wide = pl.pallas_call(
        functools.partial(exchange_kernel, planes, chunk),
        out_shape=[
            jax.ShapeDtypeStruct((2, BLOCK, chunk), bf16),
            jax.ShapeDtypeStruct((2, rows, BLOCK), bf16),
            jax.ShapeDtypeStruct((rows, LANES), f32),
        ],
        in_specs=[hbm] * 9,
        out_specs=[vmem] * 3,
        scratch_shapes=[
            pltpu.VMEM((rows, width), bf16),
            pltpu.VMEM((rows, width), bf16),
            pltpu.VMEM((2, width, 2 * hidden), bf16),
            pltpu.VMEM((2, 2 * hidden, width), bf16),
            pltpu.VMEM((3, 2 * planes, BLOCK, chunk), bf16),
            pltpu.VMEM((BLOCK, LANES), f32),
            pltpu.VMEM((BLOCK, LANES), f32),
            pltpu.VMEM((BLOCK, chunk), bf16),
            pltpu.VMEM((2 * planes * BLOCK, 2 * hidden), f32),
            pltpu.VMEM((2, planes, BLOCK, chunk), bf16),
            pltpu.VMEM((2, planes, BLOCK, chunk), f32),
            pltpu.VMEM((2, planes, BLOCK, chunk), bf16),
            pltpu.VMEM((2, planes, BLOCK, chunk), bf16),
            pltpu.VMEM((2, planes, BLOCK, chunk), bf16),
            pltpu.VMEM((2, BLOCK, chunk), f32),
            pltpu.VMEM((2, rows), jnp.int32),
            pltpu.VMEM((2, rows), f32),
            pltpu.VMEM((2, rows), jnp.int32),
            pltpu.VMEM((2, rows), f32),
            pltpu.SemaphoreType.DMA((8,)),
            pltpu.SemaphoreType.DMA((copies,)),
            pltpu.SemaphoreType.DMA((copies,)),
        ],
        compiler_params=pltpu.CompilerParams(
            collective_id=0, has_side_effects=True
        ),
    )(
        ids_forward[0].T,
        gates_forward[0].T,
        ids_backward[0].T,
        gates_backward[0].T,
        handoff[0],
        saved_inputs[0],
        cotangent[0],
        weight_in[0],
        weight_out[0],
    )
    mixed, grads = pl.pallas_call(
        functools.partial(scatter_kernel, chunk),
        out_shape=[jax.ShapeDtypeStruct((rows, width), bf16)] * 2,
        in_specs=[vmem] * 3,
        out_specs=[vmem] * 2,
    )(sums, places, gate_wide)
    return (mixed[None], grads[None])


def device_body(mesh):
    segments, experts = mesh.shape["segment"], mesh.shape["expert"]
    planes = experts // 4
    if segments == 2 and experts == GROUP and planes & (planes - 1) == 0:
        return functools.partial(exchange, planes)
    return per_device


def solution(mesh):
    return jax.shard_map(
        device_body(mesh),
        mesh=mesh,
        in_specs=(
            P("segment", "expert", None),
            P("segment", "expert", None),
            P("segment", "expert", None),
            P("segment", "expert", None),
            P("segment", "expert", None),
            P("segment", "expert", None),
            P("segment", "expert", None),
            P("segment", None, "expert"),
            P("segment", "expert", None),
        ),
        out_specs=(P("segment", "expert", None), P("segment", "expert", None)),
        check_vma=False,
    )
```

time: 47.2 us -> 43.4 us (0.919)
  local copies, waits for them, and re-layouts: 2.72 us -> 0 us
  Pallas kernels: 43.7 us -> 42.6 us
    unnamed x4 -> x0, local copies, waits for them, and re-layouts: 2.72 us -> none
    pallas_call x1 -> x2, Pallas kernels: 43.7 us -> 42.6 us  [the longest x1 40.4 us: exchange(): pl.pallas_call(functools.partial(exchange_kernel, planes, chunk), out_sha...]
where the time goes in v1:
time: 43.4 us; the launch traced here: 43.3 us
  Pallas kernels  42.6 us (98%)
  between operations  0.64 us (1%)
    pallas_call x1, Pallas kernels, exchange(): pl.pallas_call(functools.partial(exchange_kernel, planes, chunk), out_sha...  40.4 us
    pallas_call x1, Pallas kernels, exchange(): pl.pallas_call(functools.partial(scatter_kernel, chunk), out_shape=[jax.S...  2.25 us

profile of v1, /device:TPU:0, one launch (start us, length us, event | category | flops | bytes accessed | tf_op | source)
XLA Modules:
  0.0 43.3 jit_solution(15272831671505016220)
XLA Ops:
  0.6 40.4 %shard_map.104 = (bf16[2,16,1408]{2,1,0:T(8,128)(2,1)}, bf16[2,64,16]{2,1,0:T(8,128)(2,1)}, f32[64,128]{1,0:T(8,128)}) custom-call(s32[2,64]{1,0:T(2,128)} %bitcast.24, f32[2,64]{1,0:T(2,128)} %bitcast.25, s32[2,64]{1,0:T(2,128)} %bitcast.26, f32[2,64]{1,0:T(2,128)} %bitcast.27, bf16[64,4096]{1,0:T(8,128)(2,1)} %bitcast.21, bf16[64,4096]{1,0:T(8,128)(2,1)} %bitcast.22, ...), custom_call_target="tpu_custom_call" | custom-call | tf_op jit(solution)/shard_map/pallas_call | solution.py:522
  41.0 2.3 %shard_map.105 = (bf16[64,4096]{1,0:T(8,128)(2,1)}, bf16[64,4096]{1,0:T(8,128)(2,1)}) custom-call(bf16[2,16,1408]{2,1,0:T(8,128)(2,1)} %get-tuple-element.7.sums, bf16[2,64,16]{2,1,0:T(8,128)(2,1)} %get-tuple-element.8.places, f32[64,128]{1,0:T(8,128)} %get-tuple-element.9.gate_wide), custom_call_target="tpu_custom_call" | custom-call | tf_op jit(solution)/shard_map/pallas_call | solution.py:569

commit v2 on v1

--- a/solution.py
+++ b/solution.py
@@ -238,15 +238,16 @@
 
     count = [0]
     started = []
-
-    def remote(source, target, device):
+    started_inner = []
+
+    def remote(source, target, device, landing=None):
         number = count[0]
         count[0] += 1
         return pltpu.make_async_remote_copy(
             src_ref=source,
             dst_ref=target,
             send_sem=send_sem.at[number],
-            recv_sem=recv_sem.at[number],
+            recv_sem=recv_sem.at[number if landing is None else landing],
             device_id=device,
             device_id_type=MESH,
         )
@@ -254,6 +255,17 @@
     def begin(copy):
         copy.start()
         started.append(copy)
+
+    plane = expert // 4
+    inner = (plane > 0) & (plane < planes - 1)
+
+    def begin_inner(copies):
+        @pl.when(inner)
+        def _():
+            for copy in copies:
+                copy.start()
+
+        started_inner.extend(copies)
 
     tiles = chunk // LANES
     edges = [tiles * i // PARTS * LANES for i in range(PARTS + 1)]
@@ -273,14 +285,25 @@
     give_in = remote(weight_in, w_first.at[0, :, hidden : 2 * hidden], sibling)
     give_out = remote(weight_out, w_second.at[0, hidden : 2 * hidden, :], sibling)
 
-    def ship(source, target, device):
-        return [remote(source.at[:, cut], target.at[:, cut], device) for cut in cuts]
-
-    gather_z = [
-        [None] + [ship(blocks.at[kind, 0], blocks.at[kind, 2 * k], mates[k]) for k in range(1, planes)]
-        for kind in range(2)
+    def ship(source, target, device, landing=None):
+        return [
+            remote(source.at[:, cut], target.at[:, cut], device, None if landing is None else landing + part)
+            for part, cut in enumerate(cuts)
+        ]
+
+    gather_z = []
+    first_number = []
+    for kind in range(2):
+        gather_z.append(
+            [None] + [ship(blocks.at[kind, 0], blocks.at[kind, 2 * k], mates[k]) for k in range(1, planes)]
+        )
+        first_number.append(count[0] - PARTS)
+    gather_z.append([ship(late_send, blocks.at[2, 2 * k], others[k]) for k in range(planes)])
+    first_number.append(count[0] - PARTS)
+    far = planes - 1
+    forward_z = [
+        ship(blocks.at[kind, 4], blocks.at[kind, 2 * far], mates[1], first_number[kind]) for kind in range(3)
     ]
-    gather_z.append([ship(late_send, blocks.at[2, 2 * k], others[k]) for k in range(planes)])
     gather_y = [
         [ship(blocks.at[kind, 2 * k], blocks.at[kind, 2 * k + 1], across) for k in range(planes)]
         for kind in range(3)
@@ -341,29 +364,31 @@
                 )
                 target[:, start:stop] = (total * scale).astype(jnp.bfloat16)
 
+    def spread(kind):
+        for part in parts:
+            begin(gather_y[kind][0][part])
+            for k in range(1, far):
+                begin(gather_z[kind][k][part])
+        begin_inner(gather_z[kind][far])
+
     load_x.wait()
     pick(mine, rows_x, blocks.at[0, 0])
-    for part in parts:
-        begin(gather_y[0][0][part])
-        for k in range(1, planes):
-            begin(gather_z[0][k][part])
+    spread(0)
     load_s.wait()
     pick(placed_b, rows_s, blocks.at[1, 0])
-    for part in parts:
-        begin(gather_y[1][0][part])
-        for k in range(1, planes):
-            begin(gather_z[1][k][part])
+    spread(1)
     begin(give_in)
     begin(give_out)
     request.wait_recv()
     pick(req_recv[:, 0:row_count], rows_x, late_send)
     for part in parts:
-        for k in range(planes):
+        for k in range(far):
             begin(gather_z[2][k][part])
+    begin_inner(gather_z[2][far])
 
     turn = 512 if width % 512 == 0 else LANES
 
-    def transpose(low):
+    def transpose(low, share=0, shares=1):
         half = slice(low, low + hidden)
 
         def step(number, carry):
@@ -372,23 +397,33 @@
             w_second[1, half, piece] = w_first[0, piece, half].T
             return carry
 
-        lax.fori_loop(0, width // turn, step, 0)
+        steps = width // turn
+        lax.fori_loop(steps * share // shares, steps * (share + 1) // shares, step, 0)
 
     def relay(kind, k):
         for part in parts:
             gather_z[kind][k][part].wait_recv()
             begin(gather_y[kind][k][part])
+            if k == 2:
+                begin_inner([forward_z[kind][part]])
 
     load_in.wait()
     load_out.wait()
     transpose(0)
-    for k in range(1, planes):
-        relay(0, k)
+    relay(0, 1)
+    relay(0, 2)
     give_in.wait_recv()
     give_out.wait_recv()
-    transpose(hidden)
-    for k in range(1, planes):
-        relay(1, k)
+    transpose(hidden, 0, 4)
+    relay(1, 1)
+    transpose(hidden, 1, 4)
+    relay(1, 2)
+    relay(2, 0)
+    transpose(hidden, 2, 4)
+    relay(0, far)
+    transpose(hidden, 3, 4)
+    relay(1, far)
+    relay(2, 1)
     unit = jnp.where(
         lax.broadcasted_iota(jnp.int32, (row_count, row_count), 0)
         == lax.broadcasted_iota(jnp.int32, (row_count, row_count), 1),
@@ -467,17 +502,15 @@
                 z_send[o, k, :, cut] = total.astype(jnp.bfloat16)
                 begin(reduce_z[o][k][part])
 
-    relay(2, 0)
+    relay(2, 2)
     arrived(0)
     first = contract(0, segment)
-    relay(2, 1)
+    relay(2, far)
     arrived(1)
     pre = contract(1, 0)
     gate = sigmoid(pre)
     slope[...] = gate * (1.0 + pre * (1.0 - gate))
     expand(first * sigmoid(first) * (1.0 - later) + first * slope[...] * later, segment, 0)
-    for k in range(2, planes):
-        relay(2, k)
     arrived(2)
     last = contract(2, 1 - segment)
     expand(last * slope[...] * (1.0 - later) + last * sigmoid(last) * later, 1 - segment, 1)
@@ -494,6 +527,11 @@
     for copy in started:
         copy.wait_send()
 
+    @pl.when(inner)
+    def _():
+        for copy in started_inner:
+            copy.wait_send()
+
 
 def scatter_kernel(chunk, sums, places, gate_wide, out_f, out_b):
     width = out_f.shape[1]
@@ -516,15 +554,15 @@
     hidden = weight_out.shape[1]
     chunk = -(-(width // LANES) // THIRDS) * LANES
     bf16, f32 = jnp.bfloat16, jnp.float32
-    copies = 3 + PARTS * (2 * (2 * planes - 1) + 2 * planes + 2 * (2 * planes - 1))
+    copies = 3 + PARTS * (2 * (2 * planes - 1) + 2 * planes + 3 + 2 * (2 * planes - 1))
     vmem = pl.BlockSpec(memory_space=pltpu.VMEM)
     hbm = pl.BlockSpec(memory_space=pl.ANY)
     sums, places, gate_wide = pl.pallas_call(
         functools.partial(exchange_kernel, planes, chunk),
         out_shape=[
-            jax.ShapeDtypeStruct((2, BLOCK, chunk), bf16),
-            jax.ShapeDtypeStruct((2, rows, BLOCK), bf16),
-            jax.ShapeDtypeStruct((rows, LANES), f32),
+            pltpu.VMEM((2, BLOCK, chunk), bf16),
+            pltpu.VMEM((2, rows, BLOCK), bf16),
+            pltpu.VMEM((rows, LANES), f32),
         ],
         in_specs=[hbm] * 9,
         out_specs=[vmem] * 3,
@@ -571,14 +609,14 @@
         out_shape=[jax.ShapeDtypeStruct((rows, width), bf16)] * 2,
         in_specs=[vmem] * 3,
         out_specs=[vmem] * 2,
-    )(sums, places, gate_wide)
+    )(*[pltpu.with_memory_space_constraint(x, pltpu.VMEM) for x in (sums, places, gate_wide)])
     return (mixed[None], grads[None])
 
 
 def device_body(mesh):
     segments, experts = mesh.shape["segment"], mesh.shape["expert"]
     planes = experts // 4
-    if segments == 2 and experts == GROUP and planes & (planes - 1) == 0:
+    if segments == 2 and experts == GROUP and planes == 4:
         return functools.partial(exchange, planes)
     return per_device
 

time: 43.4 us -> 36.2 us (0.83)
  Pallas kernels: 42.6 us -> 35.4 us
    pallas_call x1, Pallas kernels: 40.4 us -> 34 us  [exchange(): pl.pallas_call(functools.partial(exchange_kernel, planes, chunk), out_sha...]
    pallas_call x1, Pallas kernels: 2.25 us -> 1.34 us  [exchange(): pl.pallas_call(functools.partial(scatter_kernel, chunk), out_shape=[jax.S...]
where the time goes in v2:
time: 36.2 us; the launch traced here: 36 us
  Pallas kernels  35.4 us (98%)
  between operations  0.64 us (2%)
    pallas_call x1, Pallas kernels, exchange(): pl.pallas_call(functools.partial(exchange_kernel, planes, chunk), out_sha...  34 us
    pallas_call x1, Pallas kernels, exchange(): pl.pallas_call(functools.partial(scatter_kernel, chunk), out_shape=[jax.S...  1.34 us

profile of v2, /device:TPU:0, one launch (start us, length us, event | category | flops | bytes accessed | tf_op | source)
XLA Modules:
  0.0 36.0 jit_solution(562418861921093223)
XLA Ops:
  0.6 34.0 %shard_map.104 = (bf16[2,16,1408]{2,1,0:T(8,128)(2,1)S(1)}, bf16[2,64,16]{2,1,0:T(8,128)(2,1)S(1)}, f32[64,128]{1,0:T(8,128)S(1)}) custom-call(s32[2,64]{1,0:T(2,128)} %bitcast.24, f32[2,64]{1,0:T(2,128)} %bitcast.25, s32[2,64]{1,0:T(2,128)} %bitcast.26, f32[2,64]{1,0:T(2,128)} %bitcast.27, bf16[64,4096]{1,0:T(8,128)(2,1)} %bitcast.21, ...), custom_call_target="tpu_custom_call" | custom-call | tf_op jit(solution)/shard_map/pallas_call | solution.py:560
  34.7 1.3 %shard_map.105 = (bf16[64,4096]{1,0:T(8,128)(2,1)}, bf16[64,4096]{1,0:T(8,128)(2,1)}) custom-call(bf16[2,16,1408]{2,1,0:T(8,128)(2,1)S(1)} %get-tuple-element.7.sums, bf16[2,64,16]{2,1,0:T(8,128)(2,1)S(1)} %get-tuple-element.8.places, f32[64,128]{1,0:T(8,128)S(1)} %get-tuple-element.9.gate_wide), custom_call_target="tpu_custom_call" | custom-call | tf_op jit(solution)/shard_map/pallas_call | solution.py:607

commit v3 on v2

--- a/solution.py
+++ b/solution.py
@@ -193,7 +193,8 @@
     expert = lax.axis_index("expert")
     row_count, width = rows_x.shape
     hidden = weight_out.shape[0]
-    lengths = [min(chunk, width - q * chunk) for q in range(THIRDS)]
+    tail = chunk // CAP
+    rest = THIRDS * chunk
 
     def at_expert(mask):
         return {"expert": flipped(expert, mask)}
@@ -237,84 +238,81 @@
     load_out.start()
 
     count = [0]
-    started = []
-    started_inner = []
-
-    def remote(source, target, device, landing=None):
-        number = count[0]
+
+    def landing():
         count[0] += 1
+        return recv_sem.at[count[0] - 1]
+
+    def remote(source, target, device, leaving, arriving):
         return pltpu.make_async_remote_copy(
             src_ref=source,
             dst_ref=target,
-            send_sem=send_sem.at[number],
-            recv_sem=recv_sem.at[number if landing is None else landing],
+            send_sem=leaving,
+            recv_sem=arriving,
             device_id=device,
             device_id_type=MESH,
         )
 
-    def begin(copy):
-        copy.start()
-        started.append(copy)
-
     plane = expert // 4
     inner = (plane > 0) & (plane < planes - 1)
 
-    def begin_inner(copies):
+    def start_inner(copies):
         @pl.when(inner)
         def _():
             for copy in copies:
                 copy.start()
 
-        started_inner.extend(copies)
-
-    tiles = chunk // LANES
-    edges = [tiles * i // PARTS * LANES for i in range(PARTS + 1)]
     parts = range(PARTS)
-    cuts = [slice(low, high) for low, high in zip(edges[:-1], edges[1:])]
-
-    def pieces(part):
-        low, high = edges[part], edges[part + 1]
-        middle = min(max(lengths[-1], low), high)
+    edges = [CAP * i // PARTS for i in range(PARTS + 1)]
+    cuts = [slice(tail * low, tail * high) for low, high in zip(edges[:-1], edges[1:])]
+
+    request = remote(req_send, req_recv, others[0], send_sem.at[0], landing())
+    give_in = remote(weight_in, w_first.at[0, :, hidden : 2 * hidden], sibling, send_sem.at[1], landing())
+    give_out = remote(weight_out, w_second.at[0, hidden : 2 * hidden, :], sibling, send_sem.at[2], landing())
+
+    def ship(source, target, device, leaving, arriving):
         return [
-            (start, stop, THIRDS if stop <= lengths[-1] else THIRDS - 1)
-            for start, stop in ((low, middle), (middle, high))
-            if start < stop
-        ]
-
-    request = remote(req_send, req_recv, others[0])
-    give_in = remote(weight_in, w_first.at[0, :, hidden : 2 * hidden], sibling)
-    give_out = remote(weight_out, w_second.at[0, hidden : 2 * hidden, :], sibling)
-
-    def ship(source, target, device, landing=None):
-        return [
-            remote(source.at[:, cut], target.at[:, cut], device, None if landing is None else landing + part)
+            remote(source.at[:, cut], target.at[:, cut], device, leaving, arriving[part])
             for part, cut in enumerate(cuts)
         ]
 
+    def block(kind, k, side=0):
+        return blocks.at[(kind * planes + k) * 2 + side]
+
+    far = planes - 1
+    gathers, inners, reduces = send_sem.at[3], send_sem.at[4], send_sem.at[5]
+    land_z = [[[landing() for part in parts] for k in range(planes)] for kind in range(3)]
+    land_y = [[landing()] * PARTS for kind in range(3)]
+    land_back_y = [[[landing() for part in parts] for k in range(planes)] for o in range(2)]
+    land_back_z = [[landing()] * PARTS for o in range(2)]
     gather_z = []
-    first_number = []
-    for kind in range(2):
+    for kind in range(3):
+        sources = [late_send if kind == 2 else block(kind, 0)] * planes
+        targets = others if kind == 2 else mates
         gather_z.append(
-            [None] + [ship(blocks.at[kind, 0], blocks.at[kind, 2 * k], mates[k]) for k in range(1, planes)]
+            [
+                None
+                if targets[k] is None
+                else ship(sources[k], block(kind, k), targets[k], inners if k == far else gathers, land_z[kind][k])
+                for k in range(planes)
+            ]
         )
-        first_number.append(count[0] - PARTS)
-    gather_z.append([ship(late_send, blocks.at[2, 2 * k], others[k]) for k in range(planes)])
-    first_number.append(count[0] - PARTS)
-    far = planes - 1
-    forward_z = [
-        ship(blocks.at[kind, 4], blocks.at[kind, 2 * far], mates[1], first_number[kind]) for kind in range(3)
-    ]
+    forward_z = [ship(block(kind, 2), block(kind, far), mates[1], inners, land_z[kind][far]) for kind in range(3)]
     gather_y = [
-        [ship(blocks.at[kind, 2 * k], blocks.at[kind, 2 * k + 1], across) for k in range(planes)]
+        [ship(block(kind, k), block(kind, k, 1), across, gathers, land_y[kind]) for k in range(planes)]
         for kind in range(3)
     ]
     reduce_y = [
-        [ship(y_send.at[o, k], y_recv.at[o, k], across) for k in range(planes)] for o in range(2)
+        [ship(y_send.at[o, k], y_recv.at[o, k], across, reduces, land_back_y[o][k]) for k in range(planes)]
+        for o in range(2)
     ]
     reduce_z = [
-        [None] + [ship(z_send.at[o, k], z_recv.at[o, k], mates[k]) for k in range(1, planes)]
+        [None] + [ship(z_send.at[o, k], z_recv.at[o, k], mates[k], reduces, land_back_z[o]) for k in range(1, planes)]
         for o in range(2)
     ]
+
+    def whole(number, leaving, arriving):
+        return remote(blocks.at[0:number], blocks.at[0:number], across, leaving, arriving)
 
     for table_copy in tables:
         table_copy.wait()
@@ -345,46 +343,51 @@
     mine = placed_f * (1.0 - later) + scaled_b * later
     req_send[...] = jnp.concatenate([asked, jnp.zeros((BLOCK, LANES - row_count), jnp.float32)], axis=1)
     pl.semaphore_wait(barrier, len(partners))
-    begin(request)
+    request.start()
 
     def pick(weights, rows_ref, target):
+        ending = jnp.concatenate(
+            [jnp.where(block_row == BLOCK - 1, weights[i : i + 1, :], 0.0) for i in range(CAP)], axis=0
+        )
+
+        def product(chosen, columns):
+            return jnp.dot(
+                jnp.where(chosen, 1.0, 0.0).astype(jnp.bfloat16),
+                rows_ref[:, columns],
+                preferred_element_type=jnp.float32,
+            )
+
         scale = jnp.sum(weights, axis=1, keepdims=True)
-        choose = [
-            jnp.where((weights != 0.0) & (third == q), 1.0, 0.0).astype(jnp.bfloat16) for q in range(THIRDS)
-        ]
-        for part in parts:
-            for start, stop, thirds in pieces(part):
-                total = sum(
-                    jnp.dot(
-                        choose[q],
-                        rows_ref[:, q * chunk + start : q * chunk + stop],
-                        preferred_element_type=jnp.float32,
-                    )
-                    for q in range(thirds)
-                )
-                target[:, start:stop] = (total * scale).astype(jnp.bfloat16)
+        chosen = [(weights != 0.0) & (third == q) for q in range(THIRDS)]
+        last = product(ending != 0.0, slice(rest, width)) * jnp.sum(ending, axis=1, keepdims=True)
+        for i in range(CAP):
+            total = sum(
+                product(chosen[q], slice(q * chunk + i * tail, q * chunk + (i + 1) * tail)) for q in range(THIRDS)
+            )
+            value = total * scale + last[i * BLOCK : (i + 1) * BLOCK]
+            target[:, i * tail : (i + 1) * tail] = value.astype(jnp.bfloat16)
 
     def spread(kind):
         for part in parts:
-            begin(gather_y[kind][0][part])
+            gather_y[kind][0][part].start()
             for k in range(1, far):
-                begin(gather_z[kind][k][part])
-        begin_inner(gather_z[kind][far])
+                gather_z[kind][k][part].start()
+        start_inner(gather_z[kind][far])
 
     load_x.wait()
-    pick(mine, rows_x, blocks.at[0, 0])
+    pick(mine, rows_x, block(0, 0))
     spread(0)
     load_s.wait()
-    pick(placed_b, rows_s, blocks.at[1, 0])
+    pick(placed_b, rows_s, block(1, 0))
     spread(1)
-    begin(give_in)
-    begin(give_out)
+    give_in.start()
+    give_out.start()
     request.wait_recv()
     pick(req_recv[:, 0:row_count], rows_x, late_send)
     for part in parts:
         for k in range(far):
-            begin(gather_z[2][k][part])
-    begin_inner(gather_z[2][far])
+            gather_z[2][k][part].start()
+    start_inner(gather_z[2][far])
 
     turn = 512 if width % 512 == 0 else LANES
 
@@ -403,27 +406,32 @@
     def relay(kind, k):
         for part in parts:
             gather_z[kind][k][part].wait_recv()
-            begin(gather_y[kind][k][part])
             if k == 2:
-                begin_inner([forward_z[kind][part]])
+                start_inner([forward_z[kind][part]])
+            gather_y[kind][k][part].start()
+
+    def relays(outer_order, inner_order):
+        @pl.when(inner)
+        def _():
+            for kind, k in inner_order:
+                relay(kind, k)
+
+        @pl.when(jnp.logical_not(inner))
+        def _():
+            for kind, k in outer_order:
+                relay(kind, k)
 
     load_in.wait()
     load_out.wait()
     transpose(0)
-    relay(0, 1)
-    relay(0, 2)
+    relays([(0, 1), (0, 2), (1, 1)], [(0, 1), (0, 3), (0, 2), (1, 1)])
+    relays([(2, 0)], [(1, 3), (2, 0)])
     give_in.wait_recv()
     give_out.wait_recv()
-    transpose(hidden, 0, 4)
-    relay(1, 1)
-    transpose(hidden, 1, 4)
-    relay(1, 2)
-    relay(2, 0)
-    transpose(hidden, 2, 4)
-    relay(0, far)
-    transpose(hidden, 3, 4)
-    relay(1, far)
-    relay(2, 1)
+    transpose(hidden, 0, 2)
+    relays([(1, 2), (2, 1)], [(1, 2), (2, 1)])
+    transpose(hidden, 1, 2)
+    relays([(0, 3), (2, 2), (1, 3)], [(2, 3), (2, 2)])
     unit = jnp.where(
         lax.broadcasted_iota(jnp.int32, (row_count, row_count), 0)
         == lax.broadcasted_iota(jnp.int32, (row_count, row_count), 1),
@@ -450,22 +458,22 @@
     place = lax.broadcasted_iota(jnp.int32, (batch, 2 * hidden), 0) % BLOCK
 
     def arrived(kind):
-        for part in parts:
-            for k in range(planes):
-                gather_y[kind][k][part].wait_recv()
+        whole(planes, gathers, land_y[kind][0]).wait_recv()
 
     def contract(kind, side):
-        totals = [
-            jnp.dot(
-                blocks[kind, :, :, 0 : lengths[q]].reshape(batch, lengths[q]),
-                w_first[side, q * chunk : q * chunk + lengths[q], :],
-                preferred_element_type=jnp.float32,
+        gathered = blocks[2 * planes * kind : 2 * planes * (kind + 1)].reshape(batch, chunk)
+
+        def product(columns, rows):
+            return jnp.dot(gathered[:, columns], w_first[side, rows, :], preferred_element_type=jnp.float32)
+
+        value = product(slice(0, chunk), slice(0, chunk))
+        for q in range(1, THIRDS):
+            value = value + pltpu.roll(
+                product(slice(0, chunk), slice(q * chunk, (q + 1) * chunk)), batch - CAP * q, 0
             )
-            for q in range(THIRDS)
-        ]
-        value = totals[0]
-        for q in range(1, THIRDS):
-            value = value + pltpu.roll(totals[q], batch - CAP * q, 0)
+        for i in range(CAP):
+            last = product(slice(i * tail, (i + 1) * tail), slice(rest, width))
+            value = value + jnp.where(place == i, pltpu.roll(last, batch - (BLOCK - 1 - i), 0), 0.0)
         return value
 
     def sigmoid(value):
@@ -475,21 +483,28 @@
 
     def expand(value, side, o):
         value = jnp.where(place < CAP, value, 0.0)
-        left = [pltpu.roll(value, CAP * q, 0).astype(jnp.bfloat16) if q else value.astype(jnp.bfloat16) for q in range(THIRDS)]
+        left = [value.astype(jnp.bfloat16)]
+        left += [pltpu.roll(value, CAP * q, 0).astype(jnp.bfloat16) for q in range(1, THIRDS)]
         for part in parts:
-            for start, stop, thirds in pieces(part):
+            for i in range(edges[part], edges[part + 1]):
+                piece = slice(i * tail, (i + 1) * tail)
                 total = sum(
                     jnp.dot(
                         left[q],
-                        w_second[side, :, q * chunk + start : q * chunk + stop],
+                        w_second[side, :, q * chunk + i * tail : q * chunk + (i + 1) * tail],
                         preferred_element_type=jnp.float32,
                     )
-                    for q in range(thirds)
-                ).reshape(planes, 2, BLOCK, stop - start)
-                y_keep[o, :, :, start:stop] = total[:, 0]
-                y_send[o, :, :, start:stop] = total[:, 1].astype(jnp.bfloat16)
+                    for q in range(THIRDS)
+                )
+                last = jnp.where(place == BLOCK - 1, pltpu.roll(value, BLOCK - 1 - i, 0), 0.0)
+                total = total + jnp.dot(
+                    last.astype(jnp.bfloat16), w_second[side, :, rest:width], preferred_element_type=jnp.float32
+                )
+                total = total.reshape(planes, 2, BLOCK, tail)
+                y_keep[o, :, :, piece] = total[:, 0]
+                y_send[o, :, :, piece] = total[:, 1].astype(jnp.bfloat16)
             for k in order:
-                begin(reduce_y[o][k][part])
+                reduce_y[o][k][part].start()
 
     def join(o, part):
         cut = cuts[part]
@@ -500,12 +515,11 @@
                 own_sum[o, :, cut] = total
             else:
                 z_send[o, k, :, cut] = total.astype(jnp.bfloat16)
-                begin(reduce_z[o][k][part])
-
-    relay(2, 2)
+                reduce_z[o][k][part].start()
+
     arrived(0)
     first = contract(0, segment)
-    relay(2, far)
+    relays([(2, 3)], [])
     arrived(1)
     pre = contract(1, 0)
     gate = sigmoid(pre)
@@ -518,43 +532,59 @@
         for part in parts:
             join(o, part)
     for o in range(2):
+        whole(planes - 1, reduces, land_back_z[o][0]).wait_recv()
         total = own_sum[o]
         for k in range(1, planes):
-            for part in parts:
-                reduce_z[o][k][part].wait_recv()
             total = total + z_recv[o, k].astype(jnp.float32)
         sums[segment if o == 0 else 1 - segment] = total.astype(jnp.bfloat16)
-    for copy in started:
-        copy.wait_send()
+    request.wait_send()
+    give_in.wait_send()
+    give_out.wait_send()
+    whole(5 * planes - 1, gathers, land_y[0][0]).wait_send()
+    whole(4 * planes - 2, reduces, land_y[0][0]).wait_send()
 
     @pl.when(inner)
     def _():
-        for copy in started_inner:
-            copy.wait_send()
+        whole(6, inners, land_y[0][0]).wait_send()
 
 
 def scatter_kernel(chunk, sums, places, gate_wide, out_f, out_b):
     width = out_f.shape[1]
     column = lax.broadcasted_iota(jnp.int32, places.shape[1:], 1)
     gate = gate_wide[:, 0:1]
-    for q in range(THIRDS):
-        low, high = q * chunk, min((q + 1) * chunk, width)
-        inside = (column >= CAP * q) & (column < CAP * (q + 1))
-        for i, out in enumerate([out_f, out_b]):
-            value = jnp.dot(
-                jnp.where(inside, places[i], 0.0).astype(jnp.bfloat16),
-                sums[i, :, 0 : high - low],
-                preferred_element_type=jnp.float32,
-            )
-            out[:, low:high] = (value * gate if i == 0 else value).astype(jnp.bfloat16)
+    tail = chunk // CAP
+
+    def product(i, chosen, columns):
+        return jnp.dot(chosen.astype(jnp.bfloat16), sums[i, :, columns], preferred_element_type=jnp.float32)
+
+    for i, out in enumerate([out_f, out_b]):
+        placed = places[i].astype(jnp.float32)
+
+        def put(columns, value):
+            out[:, columns] = (value * gate if i == 0 else value).astype(jnp.bfloat16)
+
+        for q in range(THIRDS):
+            inside = (column >= CAP * q) & (column < CAP * (q + 1))
+            put(slice(q * chunk, (q + 1) * chunk), product(i, jnp.where(inside, placed, 0.0), slice(0, chunk)))
+        put(
+            slice(THIRDS * chunk, width),
+            sum(
+                product(
+                    i,
+                    jnp.where(column == BLOCK - 1, placed[:, slot : slot + 1], 0.0),
+                    slice(slot * tail, (slot + 1) * tail),
+                )
+                for slot in range(CAP)
+            ),
+        )
 
 
 def exchange(planes, handoff, saved_inputs, cotangent, ids_forward, gates_forward, ids_backward, gates_backward, weight_in, weight_out):
     rows, width = handoff.shape[1:]
     hidden = weight_out.shape[1]
-    chunk = -(-(width // LANES) // THIRDS) * LANES
+    chunk = width // BLOCK * CAP
     bf16, f32 = jnp.bfloat16, jnp.float32
-    copies = 3 + PARTS * (2 * (2 * planes - 1) + 2 * planes + 3 + 2 * (2 * planes - 1))
+    landings = 3 + PARTS * 5 * planes + 5
     vmem = pl.BlockSpec(memory_space=pltpu.VMEM)
     hbm = pl.BlockSpec(memory_space=pl.ANY)
     sums, places, gate_wide = pl.pallas_call(
@@ -571,7 +601,7 @@
             pltpu.VMEM((rows, width), bf16),
             pltpu.VMEM((2, width, 2 * hidden), bf16),
             pltpu.VMEM((2, 2 * hidden, width), bf16),
-            pltpu.VMEM((3, 2 * planes, BLOCK, chunk), bf16),
+            pltpu.VMEM((6 * planes, BLOCK, chunk), bf16),
             pltpu.VMEM((BLOCK, LANES), f32),
             pltpu.VMEM((BLOCK, LANES), f32),
             pltpu.VMEM((BLOCK, chunk), bf16),
@@ -587,8 +617,8 @@
             pltpu.VMEM((2, rows), jnp.int32),
             pltpu.VMEM((2, rows), f32),
             pltpu.SemaphoreType.DMA((8,)),
-            pltpu.SemaphoreType.DMA((copies,)),
-            pltpu.SemaphoreType.DMA((copies,)),
+            pltpu.SemaphoreType.DMA((6,)),
+            pltpu.SemaphoreType.DMA((landings,)),
         ],
         compiler_params=pltpu.CompilerParams(
             collective_id=0, has_side_effects=True

time: 36.2 us -> 33.4 us (0.923)
  Pallas kernels: 35.4 us -> 32.6 us
    pallas_call x1, Pallas kernels: 34 us -> 31.4 us  [exchange(): pl.pallas_call(functools.partial(exchange_kernel, planes, chunk), out_sha...]
where the time goes in v3:
time: 33.4 us; the launch traced here: 33.3 us
  Pallas kernels  32.6 us (98%)
  between operations  0.64 us (2%)
    pallas_call x1, Pallas kernels, exchange(): pl.pallas_call(functools.partial(exchange_kernel, planes, chunk), out_sha...  31.4 us
    pallas_call x1, Pallas kernels, exchange(): pl.pallas_call(functools.partial(scatter_kernel, chunk), out_shape=[jax.S...  1.29 us

profile of v3, /device:TPU:0, one launch (start us, length us, event | category | flops | bytes accessed | tf_op | source)
XLA Modules:
  0.0 33.3 jit_solution(16493739936976262645)
XLA Ops:
  0.6 31.4 %shard_map.104 = (bf16[2,16,1280]{2,1,0:T(8,128)(2,1)S(1)}, bf16[2,64,16]{2,1,0:T(8,128)(2,1)S(1)}, f32[64,128]{1,0:T(8,128)S(1)}) custom-call(s32[2,64]{1,0:T(2,128)} %bitcast.24, f32[2,64]{1,0:T(2,128)} %bitcast.25, s32[2,64]{1,0:T(2,128)} %bitcast.26, f32[2,64]{1,0:T(2,128)} %bitcast.27, bf16[64,4096]{1,0:T(8,128)(2,1)} %bitcast.21, ...), custom_call_target="tpu_custom_call" | custom-call | tf_op jit(solution)/shard_map/pallas_call | solution.py:590
  32.0 1.3 %shard_map.105 = (bf16[64,4096]{1,0:T(8,128)(2,1)}, bf16[64,4096]{1,0:T(8,128)(2,1)}) custom-call(bf16[2,16,1280]{2,1,0:T(8,128)(2,1)S(1)} %get-tuple-element.7.sums, bf16[2,64,16]{2,1,0:T(8,128)(2,1)S(1)} %get-tuple-element.8.places, f32[64,128]{1,0:T(8,128)S(1)} %get-tuple-element.9.gate_wide), custom_call_target="tpu_custom_call" | custom-call | tf_op jit(solution)/shard_map/pallas_call | solution.py:637

commit v4 on v3

--- a/solution.py
+++ b/solution.py
@@ -140,6 +140,8 @@
 THIRDS = 3
 PARTS = 2
 LANES = 128
+GATHER_CROSS = (0,)
+REDUCE_CROSS = (0, 1)
 
 
 def flipped(position, mask):
@@ -178,6 +180,8 @@
     y_send,
     y_keep,
     y_recv,
+    cross_keep,
+    cross_recv,
     z_send,
     z_recv,
     own_sum,
@@ -208,9 +212,16 @@
     others = [at_other(k) for k in range(planes)]
 
     barrier = pltpu.get_barrier_semaphore()
-    partners = mates[1:] + others + [across, sibling]
+    plane = expert // 4
+    inner = (plane > 0) & (plane < planes - 1)
+    partners = [across, sibling, others[0]] + mates[1 : planes - 1]
     for partner in partners:
         pl.semaphore_signal(barrier, inc=1, device_id=partner, device_id_type=MESH)
+
+    @pl.when(inner)
+    def _():
+        pl.semaphore_signal(barrier, inc=1, device_id=mates[-1], device_id_type=MESH)
+
 
     tables = [
         pltpu.make_async_copy(source, target, local_sem.at[4 + i])
@@ -253,9 +264,6 @@
             device_id_type=MESH,
         )
 
-    plane = expert // 4
-    inner = (plane > 0) & (plane < planes - 1)
-
     def start_inner(copies):
         @pl.when(inner)
         def _():
@@ -283,6 +291,8 @@
     gathers, inners, reduces = send_sem.at[3], send_sem.at[4], send_sem.at[5]
     land_z = [[[landing() for part in parts] for k in range(planes)] for kind in range(3)]
     land_y = [[landing()] * PARTS for kind in range(3)]
+    land_near = [[landing() for part in parts] for kind in range(3)]
+    land_cross = [[landing() for part in parts] for o in range(2)]
     land_back_y = [[[landing() for part in parts] for k in range(planes)] for o in range(2)]
     land_back_z = [[landing()] * PARTS for o in range(2)]
     gather_z = []
@@ -299,9 +309,16 @@
         )
     forward_z = [ship(block(kind, 2), block(kind, far), mates[1], inners, land_z[kind][far]) for kind in range(3)]
     gather_y = [
-        [ship(block(kind, k), block(kind, k, 1), across, gathers, land_y[kind]) for k in range(planes)]
+        [
+            ship(block(kind, k), block(kind, k, 1), across, gathers, land_y[kind] if k else land_near[kind])
+            for k in range(planes)
+        ]
         for kind in range(3)
     ]
+    gather_cross = [
+        ship(block(kind, 0, 1), block(kind, 1, 1), mates[1], gathers, land_y[kind]) for kind in range(3)
+    ]
+    reduce_cross = [ship(y_send.at[o, 1], cross_recv.at[o], mates[1], reduces, land_cross[o]) for o in range(2)]
     reduce_y = [
         [ship(y_send.at[o, k], y_recv.at[o, k], across, reduces, land_back_y[o][k]) for k in range(planes)]
         for o in range(2)
@@ -342,7 +359,15 @@
     asked = scaled_b * (1.0 - later) + placed_f * later
     mine = placed_f * (1.0 - later) + scaled_b * later
     req_send[...] = jnp.concatenate([asked, jnp.zeros((BLOCK, LANES - row_count), jnp.float32)], axis=1)
-    pl.semaphore_wait(barrier, len(partners))
+
+    @pl.when(inner)
+    def _():
+        pl.semaphore_wait(barrier, len(partners) + 1)
+
+    @pl.when(jnp.logical_not(inner))
+    def _():
+        pl.semaphore_wait(barrier, len(partners))
+
     request.start()
 
     def pick(weights, rows_ref, target):
@@ -382,6 +407,23 @@
     spread(1)
     give_in.start()
     give_out.start()
+    turn = 512 if width % 512 == 0 else LANES
+
+    def transpose(low, share=0, shares=1):
+        half = slice(low, low + hidden)
+
+        def step(number, carry):
+            piece = pl.ds(pl.multiple_of(number * turn, turn), turn)
+            w_first[1, piece, half] = w_second[0, half, piece].T
+            w_second[1, half, piece] = w_first[0, piece, half].T
+            return carry
+
+        steps = width // turn
+        lax.fori_loop(steps * share // shares, steps * (share + 1) // shares, step, 0)
+
+    load_in.wait()
+    load_out.wait()
+    transpose(0)
     request.wait_recv()
     pick(req_recv[:, 0:row_count], rows_x, late_send)
     for part in parts:
@@ -389,26 +431,19 @@
             gather_z[2][k][part].start()
     start_inner(gather_z[2][far])
 
-    turn = 512 if width % 512 == 0 else LANES
-
-    def transpose(low, share=0, shares=1):
-        half = slice(low, low + hidden)
-
-        def step(number, carry):
-            piece = pl.ds(pl.multiple_of(number * turn, turn), turn)
-            w_first[1, piece, half] = w_second[0, half, piece].T
-            w_second[1, half, piece] = w_first[0, piece, half].T
-            return carry
-
-        steps = width // turn
-        lax.fori_loop(steps * share // shares, steps * (share + 1) // shares, step, 0)
-
     def relay(kind, k):
         for part in parts:
             gather_z[kind][k][part].wait_recv()
             if k == 2:
                 start_inner([forward_z[kind][part]])
-            gather_y[kind][k][part].start()
+            if k != 1 or part not in GATHER_CROSS:
+                gather_y[kind][k][part].start()
+
+    def cross(kind):
+        for part in parts:
+            gather_y[kind][0][part].wait_recv()
+            if part in GATHER_CROSS:
+                gather_cross[kind][part].start()
 
     def relays(outer_order, inner_order):
         @pl.when(inner)
@@ -421,17 +456,17 @@
             for kind, k in outer_order:
                 relay(kind, k)
 
-    load_in.wait()
-    load_out.wait()
-    transpose(0)
-    relays([(0, 1), (0, 2), (1, 1)], [(0, 1), (0, 3), (0, 2), (1, 1)])
-    relays([(2, 0)], [(1, 3), (2, 0)])
+    relays([(0, 1), (0, 2), (1, 1)], [(0, 1), (0, 2), (0, 3), (1, 1)])
+    cross(0)
+    cross(1)
+    relays([(2, 0)], [(1, 2), (1, 3)])
     give_in.wait_recv()
     give_out.wait_recv()
     transpose(hidden, 0, 2)
-    relays([(1, 2), (2, 1)], [(1, 2), (2, 1)])
+    relays([(1, 2), (2, 1)], [(2, 0), (2, 1)])
     transpose(hidden, 1, 2)
-    relays([(0, 3), (2, 2), (1, 3)], [(2, 3), (2, 2)])
+    relays([(0, 3), (2, 2), (1, 3)], [(2, 2), (2, 3)])
+    cross(2)
     unit = jnp.where(
         lax.broadcasted_iota(jnp.int32, (row_count, row_count), 0)
         == lax.broadcasted_iota(jnp.int32, (row_count, row_count), 1),
@@ -458,7 +493,7 @@
     place = lax.broadcasted_iota(jnp.int32, (batch, 2 * hidden), 0) % BLOCK
 
     def arrived(kind):
-        whole(planes, gathers, land_y[kind][0]).wait_recv()
+        whole(planes - 1, gathers, land_y[kind][0]).wait_recv()
 
     def contract(kind, side):
         gathered = blocks[2 * planes * kind : 2 * planes * (kind + 1)].reshape(batch, chunk)
@@ -502,20 +537,41 @@
                 )
                 total = total.reshape(planes, 2, BLOCK, tail)
                 y_keep[o, :, :, piece] = total[:, 0]
-                y_send[o, :, :, piece] = total[:, 1].astype(jnp.bfloat16)
+                y_send[o, 1:planes, :, piece] = total[1:planes, 1].astype(jnp.bfloat16)
+                if part in REDUCE_CROSS:
+                    cross_keep[o, :, piece] = total[0, 1]
+                    z_send[o, 1, :, piece] = total[1, 0].astype(jnp.bfloat16)
+                else:
+                    y_send[o, 0, :, piece] = total[0, 1].astype(jnp.bfloat16)
+            if part in REDUCE_CROSS:
+                reduce_cross[o][part].start()
             for k in order:
-                reduce_y[o][k][part].start()
+                if k > 1 or part not in REDUCE_CROSS:
+                    reduce_y[o][k][part].start()
+            if part in REDUCE_CROSS:
+                reduce_z[o][1][part].start()
 
     def join(o, part):
         cut = cuts[part]
         for k in order:
-            reduce_y[o][k][part].wait_recv()
-            total = y_keep[o, k, :, cut] + y_recv[o, k, :, cut].astype(jnp.float32)
-            if k == 0:
-                own_sum[o, :, cut] = total
-            else:
+            if k > 1 or (k == 1 and part not in REDUCE_CROSS):
+                reduce_y[o][k][part].wait_recv()
+                total = y_keep[o, k, :, cut] + y_recv[o, k, :, cut].astype(jnp.float32)
                 z_send[o, k, :, cut] = total.astype(jnp.bfloat16)
                 reduce_z[o][k][part].start()
+
+    def join_cross(o, part):
+        if part in REDUCE_CROSS:
+            cut = cuts[part]
+            reduce_cross[o][part].wait_recv()
+            total = cross_keep[o, :, cut] + cross_recv[o, :, cut].astype(jnp.float32)
+            y_send[o, 0, :, cut] = total.astype(jnp.bfloat16)
+            reduce_y[o][0][part].start()
+
+    def join_own(o, part):
+        cut = cuts[part]
+        reduce_y[o][0][part].wait_recv()
+        own_sum[o, :, cut] = y_keep[o, 0, :, cut] + y_recv[o, 0, :, cut].astype(jnp.float32)
 
     arrived(0)
     first = contract(0, segment)
@@ -531,6 +587,11 @@
     for o in range(2):
         for part in parts:
             join(o, part)
+        for part in parts:
+            join_cross(o, part)
+    for o in range(2):
+        for part in parts:
+            join_own(o, part)
     for o in range(2):
         whole(planes - 1, reduces, land_back_z[o][0]).wait_recv()
         total = own_sum[o]
@@ -584,7 +645,7 @@
     hidden = weight_out.shape[1]
     chunk = width // BLOCK * CAP
     bf16, f32 = jnp.bfloat16, jnp.float32
-    landings = 3 + PARTS * 5 * planes + 5
+    landings = 3 + PARTS * 5 * planes + 5 + PARTS * 5
     vmem = pl.BlockSpec(memory_space=pltpu.VMEM)
     hbm = pl.BlockSpec(memory_space=pl.ANY)
     sums, places, gate_wide = pl.pallas_call(
@@ -609,6 +670,8 @@
             pltpu.VMEM((2, planes, BLOCK, chunk), bf16),
             pltpu.VMEM((2, planes, BLOCK, chunk), f32),
             pltpu.VMEM((2, planes, BLOCK, chunk), bf16),
+            pltpu.VMEM((2, BLOCK, chunk), f32),
+            pltpu.VMEM((2, BLOCK, chunk), bf16),
             pltpu.VMEM((2, planes, BLOCK, chunk), bf16),
             pltpu.VMEM((2, planes, BLOCK, chunk), bf16),
             pltpu.VMEM((2, BLOCK, chunk), f32),

time: 33.4 us -> 31.9 us (0.955)
  Pallas kernels: 32.6 us -> 31.1 us
    pallas_call x1, Pallas kernels: 31.4 us -> 29.8 us  [exchange(): pl.pallas_call(functools.partial(exchange_kernel, planes, chunk), out_sha...]
where the time goes in v4:
time: 31.9 us; the launch traced here: 31.8 us
  Pallas kernels  31.1 us (97%)
  between operations  0.64 us (2%)
    pallas_call x1, Pallas kernels, exchange(): pl.pallas_call(functools.partial(exchange_kernel, planes, chunk), out_sha...  29.8 us
    pallas_call x1, Pallas kernels, exchange(): pl.pallas_call(functools.partial(scatter_kernel, chunk), out_shape=[jax.S...  1.29 us

profile of v4, /device:TPU:0, one launch (start us, length us, event | category | flops | bytes accessed | tf_op | source)
XLA Modules:
  0.0 31.8 jit_solution(8255076426608545330)
XLA Ops:
  0.6 29.8 %shard_map.104 = (bf16[2,16,1280]{2,1,0:T(8,128)(2,1)S(1)}, bf16[2,64,16]{2,1,0:T(8,128)(2,1)S(1)}, f32[64,128]{1,0:T(8,128)S(1)}) custom-call(s32[2,64]{1,0:T(2,128)} %bitcast.24, f32[2,64]{1,0:T(2,128)} %bitcast.25, s32[2,64]{1,0:T(2,128)} %bitcast.26, f32[2,64]{1,0:T(2,128)} %bitcast.27, bf16[64,4096]{1,0:T(8,128)(2,1)} %bitcast.21, ...), custom_call_target="tpu_custom_call" | custom-call | tf_op jit(solution)/shard_map/pallas_call | solution.py:651
  30.5 1.3 %shard_map.105 = (bf16[64,4096]{1,0:T(8,128)(2,1)}, bf16[64,4096]{1,0:T(8,128)(2,1)}) custom-call(bf16[2,16,1280]{2,1,0:T(8,128)(2,1)S(1)} %get-tuple-element.7.sums, bf16[2,64,16]{2,1,0:T(8,128)(2,1)S(1)} %get-tuple-element.8.places, f32[64,128]{1,0:T(8,128)S(1)} %get-tuple-element.9.gate_wide), custom_call_target="tpu_custom_call" | custom-call | tf_op jit(solution)/shard_map/pallas_call | solution.py:700

commit v5 on v4

--- a/solution.py
+++ b/solution.py
@@ -142,6 +142,7 @@
 LANES = 128
 GATHER_CROSS = (0,)
 REDUCE_CROSS = (0, 1)
+CORNER = (1, 2)
 
 
 def flipped(position, mask):
@@ -288,7 +289,7 @@
         return blocks.at[(kind * planes + k) * 2 + side]
 
     far = planes - 1
-    gathers, inners, reduces = send_sem.at[3], send_sem.at[4], send_sem.at[5]
+    gathers, inners, reduces, fars, corners = [send_sem.at[i] for i in range(3, 8)]
     land_z = [[[landing() for part in parts] for k in range(planes)] for kind in range(3)]
     land_y = [[landing()] * PARTS for kind in range(3)]
     land_near = [[landing() for part in parts] for kind in range(3)]
@@ -310,10 +311,13 @@
     forward_z = [ship(block(kind, 2), block(kind, far), mates[1], inners, land_z[kind][far]) for kind in range(3)]
     gather_y = [
         [
-            ship(block(kind, k), block(kind, k, 1), across, gathers, land_y[kind] if k else land_near[kind])
+            ship(block(kind, k), block(kind, k, 1), across, fars if k == far else gathers, land_y[kind] if k else land_near[kind])
             for k in range(planes)
         ]
         for kind in range(3)
+    ]
+    corner_z = [
+        ship(block(kind, 2), block(kind, far, 1), at_expert(6), corners, land_y[kind]) for kind in range(3)
     ]
     gather_cross = [
         ship(block(kind, 0, 1), block(kind, 1, 1), mates[1], gathers, land_y[kind]) for kind in range(3)
@@ -431,12 +435,12 @@
             gather_z[2][k][part].start()
     start_inner(gather_z[2][far])
 
-    def relay(kind, k):
+    def relay(kind, k, corner=False):
         for part in parts:
             gather_z[kind][k][part].wait_recv()
             if k == 2:
-                start_inner([forward_z[kind][part]])
-            if k != 1 or part not in GATHER_CROSS:
+                start_inner([forward_z[kind][part]] + ([corner_z[kind][part]] if kind in CORNER else []))
+            if not corner and (k != 1 or part not in GATHER_CROSS):
                 gather_y[kind][k][part].start()
 
     def cross(kind):
@@ -454,18 +458,18 @@
         @pl.when(jnp.logical_not(inner))
         def _():
             for kind, k in outer_order:
-                relay(kind, k)
+                relay(kind, k, k == far and kind in CORNER)
 
     relays([(0, 1), (0, 2), (1, 1)], [(0, 1), (0, 2), (0, 3), (1, 1)])
     cross(0)
     cross(1)
-    relays([(2, 0)], [(1, 2), (1, 3)])
+    relays([(2, 0)], [(1, 2), (2, 0), (1, 3)])
     give_in.wait_recv()
     give_out.wait_recv()
     transpose(hidden, 0, 2)
-    relays([(1, 2), (2, 1)], [(2, 0), (2, 1)])
+    relays([(1, 2), (2, 1)], [(2, 1)])
     transpose(hidden, 1, 2)
-    relays([(0, 3), (2, 2), (1, 3)], [(2, 2), (2, 3)])
+    relays([(0, 3), (2, 2)], [(2, 2), (2, 3)])
     cross(2)
     unit = jnp.where(
         lax.broadcasted_iota(jnp.int32, (row_count, row_count), 0)
@@ -575,12 +579,13 @@
 
     arrived(0)
     first = contract(0, segment)
-    relays([(2, 3)], [])
+    relays([(1, 3)], [])
     arrived(1)
     pre = contract(1, 0)
     gate = sigmoid(pre)
     slope[...] = gate * (1.0 + pre * (1.0 - gate))
     expand(first * sigmoid(first) * (1.0 - later) + first * slope[...] * later, segment, 0)
+    relays([(2, 3)], [])
     arrived(2)
     last = contract(2, 1 - segment)
     expand(last * slope[...] * (1.0 - later) + last * sigmoid(last) * later, 1 - segment, 1)
@@ -601,12 +606,20 @@
     request.wait_send()
     give_in.wait_send()
     give_out.wait_send()
-    whole(5 * planes - 1, gathers, land_y[0][0]).wait_send()
+    whole(5 * planes - 4, gathers, land_y[0][0]).wait_send()
     whole(4 * planes - 2, reduces, land_y[0][0]).wait_send()
 
     @pl.when(inner)
     def _():
         whole(6, inners, land_y[0][0]).wait_send()
+        whole(3, fars, land_y[0][0]).wait_send()
+        if CORNER:
+            whole(len(CORNER), corners, land_y[0][0]).wait_send()
+
+    @pl.when(jnp.logical_not(inner))
+    def _():
+        if len(CORNER) < 3:
+            whole(3 - len(CORNER), fars, land_y[0][0]).wait_send()
 
 
 def scatter_kernel(chunk, sums, places, gate_wide, out_f, out_b):
@@ -680,7 +693,7 @@
             pltpu.VMEM((2, rows), jnp.int32),
             pltpu.VMEM((2, rows), f32),
             pltpu.SemaphoreType.DMA((8,)),
-            pltpu.SemaphoreType.DMA((6,)),
+            pltpu.SemaphoreType.DMA((8,)),
             pltpu.SemaphoreType.DMA((landings,)),
         ],
         compiler_params=pltpu.CompilerParams(

time: 31.9 us -> 31.1 us (0.975)
  Pallas kernels: 31.1 us -> 30.3 us
    pallas_call x1, Pallas kernels: 29.8 us -> 29 us  [exchange(): pl.pallas_call(functools.partial(exchange_kernel, planes, chunk), out_sha...]
where the time goes in v5:
time: 31.1 us; the launch traced here: 30.9 us
  Pallas kernels  30.3 us (97%)
  between operations  0.64 us (2%)
    pallas_call x1, Pallas kernels, exchange(): pl.pallas_call(functools.partial(exchange_kernel, planes, chunk), out_sha...  29 us
    pallas_call x1, Pallas kernels, exchange(): pl.pallas_call(functools.partial(scatter_kernel, chunk), out_shape=[jax.S...  1.29 us

profile of v5, /device:TPU:0, one launch (start us, length us, event | category | flops | bytes accessed | tf_op | source)
XLA Modules:
  0.0 30.9 jit_solution(10374933011460237040)
XLA Ops:
  0.6 29.0 %shard_map.104 = (bf16[2,16,1280]{2,1,0:T(8,128)(2,1)S(1)}, bf16[2,64,16]{2,1,0:T(8,128)(2,1)S(1)}, f32[64,128]{1,0:T(8,128)S(1)}) custom-call(s32[2,64]{1,0:T(2,128)} %bitcast.24, f32[2,64]{1,0:T(2,128)} %bitcast.25, s32[2,64]{1,0:T(2,128)} %bitcast.26, f32[2,64]{1,0:T(2,128)} %bitcast.27, bf16[64,4096]{1,0:T(8,128)(2,1)} %bitcast.21, ...), custom_call_target="tpu_custom_call" | custom-call | tf_op jit(solution)/shard_map/pallas_call | solution.py:664
  29.6 1.3 %shard_map.105 = (bf16[64,4096]{1,0:T(8,128)(2,1)}, bf16[64,4096]{1,0:T(8,128)(2,1)}) custom-call(bf16[2,16,1280]{2,1,0:T(8,128)(2,1)S(1)} %get-tuple-element.7.sums, bf16[2,64,16]{2,1,0:T(8,128)(2,1)S(1)} %get-tuple-element.8.places, f32[64,128]{1,0:T(8,128)S(1)} %get-tuple-element.9.gate_wide), custom_call_target="tpu_custom_call" | custom-call | tf_op jit(solution)/shard_map/pallas_call | solution.py:713

commit v6 on v5

--- a/solution.py
+++ b/solution.py
@@ -589,11 +589,24 @@
     arrived(2)
     last = contract(2, 1 - segment)
     expand(last * slope[...] * (1.0 - later) + last * sigmoid(last) * later, 1 - segment, 1)
-    for o in range(2):
+    for part in parts:
+        join(0, part)
+
+    @pl.when(jnp.logical_not(inner))
+    def _():
         for part in parts:
-            join(o, part)
+            join_cross(0, part)
+
+    for part in parts:
+        join(1, part)
+
+    @pl.when(inner)
+    def _():
         for part in parts:
-            join_cross(o, part)
+            join_cross(0, part)
+
+    for part in parts:
+        join_cross(1, part)
     for o in range(2):
         for part in parts:
             join_own(o, part)
@@ -622,24 +635,33 @@
             whole(3 - len(CORNER), fars, land_y[0][0]).wait_send()
 
 
-def scatter_kernel(chunk, sums, places, gate_wide, out_f, out_b):
+def scatter_kernel(chunk, sums, places, gate_wide, mixed, grads, out_f, out_b, sems):
     width = out_f.shape[1]
     column = lax.broadcasted_iota(jnp.int32, places.shape[1:], 1)
     gate = gate_wide[:, 0:1]
     tail = chunk // CAP
+    copies = []
 
     def product(i, chosen, columns):
         return jnp.dot(chosen.astype(jnp.bfloat16), sums[i, :, columns], preferred_element_type=jnp.float32)
 
-    for i, out in enumerate([out_f, out_b]):
+    for i, (held, out) in enumerate([(out_f, mixed), (out_b, grads)]):
         placed = places[i].astype(jnp.float32)
 
         def put(columns, value):
-            out[:, columns] = (value * gate if i == 0 else value).astype(jnp.bfloat16)
+            held[:, columns] = (value * gate if i == 0 else value).astype(jnp.bfloat16)
+
+        def send(columns):
+            copies.append(
+                pltpu.make_async_copy(held.at[:, columns], out.at[:, columns], sems.at[len(copies)])
+            )
+            copies[-1].start()
 
         for q in range(THIRDS):
             inside = (column >= CAP * q) & (column < CAP * (q + 1))
             put(slice(q * chunk, (q + 1) * chunk), product(i, jnp.where(inside, placed, 0.0), slice(0, chunk)))
+            if q < THIRDS - 1:
+                send(slice(q * chunk, (q + 1) * chunk))
         put(
             slice(THIRDS * chunk, width),
             sum(
@@ -651,6 +673,9 @@
                 for slot in range(CAP)
             ),
         )
+        send(slice((THIRDS - 1) * chunk, width))
+    for copy in copies:
+        copy.wait()
 
 
 def exchange(planes, handoff, saved_inputs, cotangent, ids_forward, gates_forward, ids_backward, gates_backward, weight_in, weight_out):
@@ -714,7 +739,12 @@
         functools.partial(scatter_kernel, chunk),
         out_shape=[jax.ShapeDtypeStruct((rows, width), bf16)] * 2,
         in_specs=[vmem] * 3,
-        out_specs=[vmem] * 2,
+        out_specs=[hbm] * 2,
+        scratch_shapes=[
+            pltpu.VMEM((rows, width), bf16),
+            pltpu.VMEM((rows, width), bf16),
+            pltpu.SemaphoreType.DMA((2 * THIRDS,)),
+        ],
     )(*[pltpu.with_memory_space_constraint(x, pltpu.VMEM) for x in (sums, places, gate_wide)])
     return (mixed[None], grads[None])
 

time: 31.1 us -> 31 us (level)
  no operation moved by 1% of the time
where the time goes in v6:
time: 31 us; the launch traced here: 30.9 us
  Pallas kernels  30.2 us (97%)
  between operations  0.64 us (2%)
    pallas_call x1, Pallas kernels, exchange(): pl.pallas_call(functools.partial(exchange_kernel, planes, chunk), out_sha...  29 us
    pallas_call x1, Pallas kernels, exchange(): pl.pallas_call(functools.partial(scatter_kernel, chunk), out_shape=[jax.S...  1.24 us

profile of v6, /device:TPU:0, one launch (start us, length us, event | category | flops | bytes accessed | tf_op | source)
XLA Modules:
  0.0 30.9 jit_solution(6505591106690887932)
XLA Ops:
  0.6 29.0 %shard_map.104 = (bf16[2,16,1280]{2,1,0:T(8,128)(2,1)S(1)}, bf16[2,64,16]{2,1,0:T(8,128)(2,1)S(1)}, f32[64,128]{1,0:T(8,128)S(1)}) custom-call(s32[2,64]{1,0:T(2,128)} %bitcast.24, f32[2,64]{1,0:T(2,128)} %bitcast.25, s32[2,64]{1,0:T(2,128)} %bitcast.26, f32[2,64]{1,0:T(2,128)} %bitcast.27, bf16[64,4096]{1,0:T(8,128)(2,1)} %bitcast.21, ...), custom_call_target="tpu_custom_call" | custom-call | tf_op jit(solution)/shard_map/pallas_call | solution.py:689
  29.6 1.2 %shard_map.105 = (bf16[64,4096]{1,0:T(8,128)(2,1)}, bf16[64,4096]{1,0:T(8,128)(2,1)}) custom-call(bf16[2,16,1280]{2,1,0:T(8,128)(2,1)S(1)} %get-tuple-element.7.sums, bf16[2,64,16]{2,1,0:T(8,128)(2,1)S(1)} %get-tuple-element.8.places, f32[64,128]{1,0:T(8,128)S(1)} %get-tuple-element.9.gate_wide), custom_call_target="tpu_custom_call" | custom-call | tf_op jit(solution)/shard_map/pallas_call | solution.py:738
